TPU v7x, 32 devices: a whole 2x2x4 slice. The times are simulated.
32 devices in a mesh: groups: 2 (over x), sector: 16 (over z, y, core).
Axes of the slice: x: 2, y: 2, z: 4, core: 2. Of those that a mesh axis runs over, the one named last changes fastest.
Arguments:
- fields: bfloat16 [524288, 128], P(('groups', 'sector')), parts along dimension 0, may hold values from -6 to 6
- weights: bfloat16 [5120, 128, 128], P('sector'), may hold values from -0.25 to 0.25
- source_block: int32 [5120], P('sector'), may hold values from 0 to 127
- target_block: int32 [1280], P('sector'), may hold values from 0 to 1023, as said below
- area: float32 [131072], P('sector'), may hold values from 0.1 to 1
Outputs:
- level10: bfloat16 [262144, 128], P(('groups', 'sector')), parts along dimension 0
- level9: float32 [65536, 128], P(('groups', 'sector')), parts along dimension 0
- level8: float32 [16384, 128], P(('groups', 'sector')), parts along dimension 0
There are 2 independent parts, one for each index of `groups`. A program takes and returns all parts, laid end to end along the dimension named above; an argument that names none is the same for every part. Nothing has to cross between parts.
Inputs may be any that keep to these rules, and one draw needn't show every extreme that they name: `target_block`: the partial blocks of one sector s (indices s * 80 to s * 80 + 79) name distinct target blocks; each target block b lies in sector b // 64, at most 2 sectors from s around the closed loop; at most 16 of them lie in any one sector other than s, and every sector has exactly 16 in one other sector.
All inputs are finite; a program needn't handle non-finite values.
Results may differ from a plain program's by a relative error of at most 0.0075.
Values may be sent and summed in bfloat16 or wider, within the bound.
A program may use at most 128 MiB of HBM per device.

v0:
```python
import jax
import jax.numpy as jnp
from jax import lax
from jax.sharding import PartitionSpec as P

REACH = 2


def shifted(block, axis, distance):
    devices = range(lax.axis_size(axis))
    route = [((i - distance) % len(devices), i) for i in devices]
    return lax.ppermute(block, axis, route)


def place_blocks(slot_ids, selected, partial_value, owned):
    onehot = ((slot_ids[None, :] == jnp.arange(owned)[:, None]) & selected[None, :]).astype(
        jnp.bfloat16
    )
    return jnp.einsum("tg,gpc->tpc", onehot, partial_value, preferred_element_type=jnp.float32)


def per_device(fields, weights, source_block, target_block, area):
    width_blk = weights.shape[1]
    cols = fields.shape[1]
    owned = area.shape[0] // width_blk
    groups_dev = target_block.shape[0]
    per_group = weights.shape[0] // groups_dev
    sectors = lax.axis_size("sector")
    myself = lax.axis_index("sector")
    source_blocks = fields.reshape(-1, width_blk, cols)
    picked = source_blocks[source_block]
    terms = jnp.einsum("kps,ksc->kpc", weights, picked, preferred_element_type=jnp.float32)
    partial_value = (
        terms.reshape(groups_dev, per_group, width_blk, cols).sum(1).astype(jnp.bfloat16)
    )
    owner_sector = target_block // owned
    slot_local = target_block % owned
    distance = (owner_sector - myself + sectors) % sectors
    distance = jnp.where(distance > sectors // 2, distance - sectors, distance)
    summed = place_blocks(slot_local, distance == 0, partial_value, owned)
    carry_right = jnp.zeros_like(summed)
    carry_left = jnp.zeros_like(summed)
    for reach_step in range(REACH, 0, -1):
        carry_right = carry_right + place_blocks(
            slot_local, distance == reach_step, partial_value, owned
        )
        carry_right = shifted(carry_right.astype(jnp.bfloat16), "sector", 1).astype(
            carry_right.dtype
        )
        carry_left = carry_left + place_blocks(
            slot_local, distance == -reach_step, partial_value, owned
        )
        carry_left = shifted(carry_left.astype(jnp.bfloat16), "sector", -1).astype(carry_left.dtype)
    summed = summed + carry_right + carry_left
    flat = summed.reshape(-1, cols)
    level10 = flat.astype(jnp.bfloat16)
    weighted = flat * area[:, None]
    area_nine = area.reshape(-1, 4).sum(1)
    sums_nine = weighted.reshape(-1, 4, cols).sum(1)
    level9 = sums_nine / area_nine[:, None]
    level8 = sums_nine.reshape(-1, 4, cols).sum(1) / area_nine.reshape(-1, 4).sum(1)[:, None]
    return (level10, level9, level8)


def solution(mesh):
    in_specs = (
        P(("groups", "sector"), None),
        P("sector", None, None),
        P("sector"),
        P("sector"),
        P("sector"),
    )
    out_specs = (
        P(("groups", "sector"), None),
        P(("groups", "sector"), None),
        P(("groups", "sector"), None),
    )
    return jax.shard_map(
        per_device, mesh=mesh, in_specs=in_specs, out_specs=out_specs, check_vma=False
    )
```

profile of v0, /device:TPU:1, one launch (start us, length us, event | category | flops | bytes accessed | tf_op | source)
XLA Modules:
  0.0 169.3 jit_solution(10889706128078868953)
XLA Ops:
  0.6 0.7 compare_select_fusion
  1.3 12.9 %gather_fusion = bf16[320,128,128]{2,1,0:T(8,128)(2,1)} fusion(bf16[128,128,128]{2,1,0:T(8,128)(2,1)} %bitcast.34, s32[1024]{0:T(1024)S(1)} %pad_clamp_fusion), kind=kCustom, calls=%fused_computation | custom fusion | bytes 20972800 | tf_op jit(solution)/shard_map/gather | solution.py:31
  14.3 15.5 %fusion.34 = f32[320,128,128]{2,1,0:T(8,128)} fusion(bf16[320,128,128]{2,1,0:T(8,128)(2,1)} %gather_fusion, bf16[320,128,128]{2,1,0:T(8,128)(2,1)} %param.6), kind=kOutput, calls=%fused_computation.51 | convolution fusion | flops 1342177280 | bytes 41943040 | tf_op jit(solution)/shard_map/kps,ksc->kpc/dot_general | solution.py:32
  29.8 10.3 %reduce_sum.45 = bf16[80,128,128]{1,2,0:T(8,128)(2,1)} reduce(f32[80,4,128,128]{2,3,1,0:T(8,128)} %bitcast.33, f32[]{:T(128)} %constant.57.clone.1), dimensions={1}, to_apply=%region_0.0 | reduce | flops 3932160 | bytes 23592964 | tf_op jit(solution)/shard_map/reduce_sum | solution.py:34
  40.1 0.0 copy-start.2
  40.1 3.7 %copy.12 = bf16[80,128,128]{2,0,1:T(8,128)(2,1)S(1)} copy(bf16[80,128,128]{1,2,0:T(8,128)(2,1)} %reduce_sum.45) | data formatting | bytes 5242880 | tf_op jit(solution)/shard_map/convert_element_type | solution.py:34
  43.9 0.0 copy-done.2
  43.9 0.7 convolution_convert_fusion
  44.6 0.1 collective-permute-start.2
  44.7 0.7 convolution_convert_fusion.1
  45.4 2.6 %collective-permute-start = (bf16[64,128,128]{2,0,1:T(8,128)(2,1)S(1)}, bf16[64,128,128]{2,0,1:T(8,128)(2,1)S(1)}, u32[]{:S(2)}, u32[]{:S(2)}) collective-permute-start(bf16[64,128,128]{2,0,1:T(8,128)(2,1)S(1)} %convolution_convert_fusion.1), channel_id=1, source_target_pairs={{15,0},{0,1},{1,2},{2,3},{3,4},{4,5},{5,6},{6,7},{7,8},{8,9},{9,10... | collective-permute-start | bytes 6291464 | tf_op jit(solution)/shard_map/ppermute | solution.py:12
  48.0 45.4 %collective-permute-done.2 = bf16[64,128,128]{2,0,1:T(8,128)(2,1)S(1)} collective-permute-done((bf16[64,128,128]{2,0,1:T(8,128)(2,1)S(1)}, bf16[64,128,128]{2,0,1:T(8,128)(2,1)S(1)}, u32[]{:S(2)}, u32[]{:S(2)}) %collective-permute-start.2) | collective-permute-done | bytes 2097184 | tf_op jit(solution)/shard_map/ppermute | solution.py:12
  93.5 2.0 %add_convert_fusion = bf16[64,128,128]{2,0,1:T(8,128)(2,1)} fusion(bf16[64,128,128]{2,0,1:T(8,128)(2,1)S(1)} %collective-permute-done.2, bf16[80,128,128]{2,0,1:T(8,128)(2,1)S(1)} %copy.12, s32[80]{0:T(128)S(1)} %and_select_fusion.2, pred[80]{0:T(512)(128)(4,1)S(1)} %get-tuple-element.9), kind=kOutput, calls=%fused_computation.3 | convolution fusion | flops 170928128 | bytes 6816144 | tf_op jit(solution)/shard_map/tg,gpc->tpc/dot_general | solution.py:19
  95.5 0.0 collective-permute-start.3
  95.5 20.4 %collective-permute-done = bf16[64,128,128]{2,0,1:T(8,128)(2,1)S(1)} collective-permute-done((bf16[64,128,128]{2,0,1:T(8,128)(2,1)S(1)}, bf16[64,128,128]{2,0,1:T(8,128)(2,1)S(1)}, u32[]{:S(2)}, u32[]{:S(2)}) %collective-permute-start) | collective-permute-done | bytes 2097184 | tf_op jit(solution)/shard_map/ppermute | solution.py:12
  116.0 0.0 copy-start.1
  116.0 2.0 %add_convert_fusion.1 = bf16[64,128,128]{2,0,1:T(8,128)(2,1)} fusion(bf16[64,128,128]{2,0,1:T(8,128)(2,1)S(1)} %collective-permute-done, bf16[80,128,128]{2,0,1:T(8,128)(2,1)S(1)} %copy.12, s32[80]{0:T(128)S(1)} %and_select_fusion.2, pred[80]{0:T(512)(128)(4,1)S(1)} %get-tuple-element.5), kind=kOutput, calls=%fused_computation.4 | convolution fusion | flops 170928128 | bytes 6816144 | tf_op jit(solution)/shard_map/tg,gpc->tpc/dot_general | solution.py:19
  118.0 2.5 %collective-permute-start.1 = (bf16[64,128,128]{2,0,1:T(8,128)(2,1)}, bf16[64,128,128]{2,0,1:T(8,128)(2,1)}, u32[]{:S(2)}, u32[]{:S(2)}) collective-permute-start(bf16[64,128,128]{2,0,1:T(8,128)(2,1)} %add_convert_fusion.1), channel_id=1, source_target_pairs={{15,0},{0,1},{1,2},{2,3},{3,4},{4,5},{5,6},{6,7},{7,8},{8,9},{9,10... | collective-permute-start | bytes 6291464 | tf_op jit(solution)/shard_map/ppermute | solution.py:12
  120.5 0.0 copy-done.1
  120.5 2.0 %mul.11 = f32[2048,4]{1,0:T(8,128)} reshape(f32[8192]{0:T(1024)S(1)} %copy-done.1) | data formatting | bytes 65536 | tf_op jit(solution)/shard_map/mul | solution.py:57
  122.5 1.6 reduce_sum.47
  124.1 0.3 reshape.43
  124.4 0.1 reduce_sum.49
  124.5 0.7 fusion.6
  125.2 18.5 %collective-permute-done.3 = bf16[64,128,128]{2,0,1:T(8,128)(2,1)} collective-permute-done((bf16[64,128,128]{2,0,1:T(8,128)(2,1)}, bf16[64,128,128]{2,0,1:T(8,128)(2,1)}, u32[]{:S(2)}, u32[]{:S(2)}) %collective-permute-start.3) | collective-permute-done | bytes 2097184 | tf_op jit(solution)/shard_map/ppermute | solution.py:12
  143.8 0.0 collective-permute-done.1
  143.8 4.8 %fusion.33 = (bf16[64,128,128]{2,0,1:T(8,128)(2,1)}, f32[64,128,128]{2,0,1:T(8,128)S(1)}) fusion(bf16[64,128,128]{2,0,1:T(8,128)(2,1)} %collective-permute-done.3, f32[64,128,128]{2,0,1:T(8,128)S(1)} %fusion.6, bf16[64,128,128]{2,0,1:T(8,128)(2,1)} %collective-permute-done.1), kind=kLoop, calls=%fused_computation.50 | loop fusion | flops 5242880 | bytes 14680064 | tf_op jit(solution)/shard_map/convert_element_type | solution.py:56
  148.6 0.0 copy-start
  148.6 2.4 %copy.18 = f32[64,128,128]{2,1,0:T(8,128)S(1)} copy(f32[64,128,128]{2,0,1:T(8,128)S(1)} %get-tuple-element.4) | data formatting | bytes 8388608 | tf_op jit(solution)/shard_map/add | solution.py:54
  151.0 0.0 copy-done
  151.1 11.2 %multiply_reduce_fusion = f32[2048,128]{1,0:T(8,128)S(1)} fusion(f32[2048,4,128]{2,1,0:T(4,128)S(1)} %bitcast.35, f32[2048,4]{1,0:T(8,128)S(1)} %copy-done), kind=kLoop, calls=%fused_computation.1 | loop fusion | flops 1835008 | bytes 5275648 | tf_op jit(solution)/shard_map/reduce_sum | solution.py:59
  162.3 1.3 broadcast_divide_fusion
  163.6 0.6 reduce_sum.48
  164.2 4.3 %copy.17 = bf16[64,128,128]{2,1,0:T(8,128)(2,1)} copy(bf16[64,128,128]{2,0,1:T(8,128)(2,1)} %get-tuple-element.3) | data formatting | bytes 4194304 | tf_op jit(solution)/shard_map/convert_element_type | solution.py:56
  168.5 0.8 broadcast_divide_fusion.1
  (4 shorter events, 0.1 us)
Async XLA Ops:
  40.1 3.8 %copy-start.2 = (s32[80]{0:T(128)S(1)}, s32[80]{0:T(128)}, u32[]{:S(2)}) copy-start(s32[80]{0:T(128)} %param.8) | copy-start | bytes 964
  44.6 48.9 %collective-permute-start.2 = (bf16[64,128,128]{2,0,1:T(8,128)(2,1)S(1)}, bf16[64,128,128]{2,0,1:T(8,128)(2,1)S(1)}, u32[]{:S(2)}, u32[]{:S(2)}) collective-permute-start(bf16[64,128,128]{2,0,1:T(8,128)(2,1)S(1)} %convolution_convert_fusion), channel_id=1, source_target_pairs={{1,0},{2,1},{3,2},{4,3},{5,4},{6,5},{7,6},{8,7},{9,8},{10,9},{11,1... | collective-permute-start | bytes 6291464 | tf_op jit(solution)/shard_map/ppermute | solution.py:12
  45.4 70.5 %collective-permute-start = (bf16[64,128,128]{2,0,1:T(8,128)(2,1)S(1)}, bf16[64,128,128]{2,0,1:T(8,128)(2,1)S(1)}, u32[]{:S(2)}, u32[]{:S(2)}) collective-permute-start(bf16[64,128,128]{2,0,1:T(8,128)(2,1)S(1)} %convolution_convert_fusion.1), channel_id=1, source_target_pairs={{15,0},{0,1},{1,2},{2,3},{3,4},{4,5},{5,6},{6,7},{7,8},{8,9},{9,10... | collective-permute-start | bytes 6291464 | tf_op jit(solution)/shard_map/ppermute | solution.py:12
  95.5 48.2 %collective-permute-start.3 = (bf16[64,128,128]{2,0,1:T(8,128)(2,1)}, bf16[64,128,128]{2,0,1:T(8,128)(2,1)}, u32[]{:S(2)}, u32[]{:S(2)}) collective-permute-start(bf16[64,128,128]{2,0,1:T(8,128)(2,1)} %add_convert_fusion), channel_id=1, source_target_pairs={{1,0},{2,1},{3,2},{4,3},{5,4},{6,5},{7,6},{8,7},{9,8},{10,9},{11,1... | collective-permute-start | bytes 6291464 | tf_op jit(solution)/shard_map/ppermute | solution.py:12
  116.0 4.5 %copy-start.1 = (f32[8192]{0:T(1024)S(1)}, f32[8192]{0:T(1024)}, u32[]{:S(2)}) copy-start(f32[8192]{0:T(1024)} %param.9) | copy-start | bytes 98308
  118.0 25.8 %collective-permute-start.1 = (bf16[64,128,128]{2,0,1:T(8,128)(2,1)}, bf16[64,128,128]{2,0,1:T(8,128)(2,1)}, u32[]{:S(2)}, u32[]{:S(2)}) collective-permute-start(bf16[64,128,128]{2,0,1:T(8,128)(2,1)} %add_convert_fusion.1), channel_id=1, source_target_pairs={{15,0},{0,1},{1,2},{2,3},{3,4},{4,5},{5,6},{6,7},{7,8},{8,9},{9,10... | collective-permute-start | bytes 6291464 | tf_op jit(solution)/shard_map/ppermute | solution.py:12
  148.6 2.4 %copy-start = (f32[2048,4]{1,0:T(8,128)S(1)}, f32[2048,4]{1,0:T(8,128)}, u32[]{:S(2)}) copy-start(f32[2048,4]{1,0:T(8,128)} %mul.11) | copy-start | bytes 98308
where the time goes:
time: 170 us; the launch traced here: 169 us
  waiting for transfers between devices  84.4 us (50%)
  other arithmetic  31.6 us (19%)
  local copies, waits for them, and re-layouts  25.7 us (15%)
  matrix products  21.7 us (13%)
  starting transfers between devices  5.22 us (3%)
    ppermute x4, waiting for transfers between devices, shifted(): return lax.ppermute(block, axis, route)  84.4 us
    dot_general x1, matrix products, per_device(): jnp.einsum('kps,ksc->kpc', weights, picked, preferred_element_type=jnp.fl...  15.5 us
    gather x1, local copies, waits for them, and re-layouts, per_device(): picked = source_blocks[source_block]  12.9 us
    reduce_sum x1, other arithmetic, per_device(): sums_nine = weighted.reshape(-1, 4, cols).sum(1)  11.2 us
    reduce_sum x1, other arithmetic, per_device(): terms.reshape(groups_dev, per_group, width_blk, cols).sum(1)  10.3 us
    dot_general x5, matrix products, place_blocks(): jnp.einsum('tg,gpc->tpc', onehot, partial_value, preferred_element_type=j...  6.15 us
    ppermute x4, starting transfers between devices, shifted(): return lax.ppermute(block, axis, route)  5.22 us
    convert_element_type x1, other arithmetic, per_device(): level10 = flat.astype(jnp.bfloat16)  4.82 us
  transfers between devices with their start and end apart: 4, of which 3 were waited for; matrix products, arithmetic and copies ran while one was open for 6% of the time, Pallas kernels for 0%

commit v1 on v0

v1 whole, which is shorter than its diff:
```python
import functools

import jax
import jax.numpy as jnp
from jax import lax
from jax.experimental import pallas as pl
from jax.experimental.pallas import tpu as pltpu
from jax.sharding import PartitionSpec as P

CAP = 16
MOVES = (2, -2, 1, -1)
CHUNK = 8


def shifted(block, axis, distance):
    size = lax.axis_size(axis)
    route = [((i - distance) % size, i) for i in range(size)]
    return lax.ppermute(block, axis, route)


def remap_kernel(
    sectors, owned, per_group, source, target, w_hbm, f_hbm, *rest
):
    sends = rest[:4]
    own_out, wbuf, fbuf, obuf, count, w_sem, f_sem, o_sem = rest[4:]
    groups_dev = target.shape[0]
    chunks = groups_dev // CHUNK
    per_chunk = CHUNK * per_group
    f_copy = pltpu.make_async_copy(f_hbm, fbuf, f_sem)
    f_copy.start()

    def w_copy(c):
        rows = pl.ds(c * per_chunk, per_chunk)
        return pltpu.make_async_copy(w_hbm.at[rows], wbuf.at[rows], w_sem.at[c])

    for c in range(chunks):
        w_copy(c).start()
    me = lax.axis_index("sector")
    for k in range(4):
        count[k] = 0

    @pl.loop(0, owned)
    def _(t):
        obuf[t] = jnp.zeros(obuf.shape[1:], obuf.dtype)

    f_copy.wait()

    @pl.loop(0, chunks)
    def _(c):
        w_copy(c).wait()
        for p in range(CHUNK):
            g = c * CHUNK + p
            first = g * per_group
            left = jnp.concatenate([wbuf[first + q] for q in range(per_group)], axis=1)
            right = jnp.concatenate(
                [fbuf[source[first + q]] for q in range(per_group)], axis=0
            )
            value = jnp.dot(left, right, preferred_element_type=jnp.float32)
            where_to = target[g]
            distance = lax.rem(where_to // owned - me + sectors, sectors)
            mine = distance == 0
            kind = jnp.where(
                distance == 2, 0, jnp.where(distance == 1, 2, jnp.where(distance == sectors - 1, 3, 1))
            )
            rank = count[kind]
            count[kind] = rank + jnp.where(mine, 0, 1)
            slot = jnp.where(mine, lax.rem(where_to, owned), owned + CAP * kind + rank)
            obuf[slot] = value.astype(obuf.dtype)

    copies = [
        pltpu.make_async_copy(obuf.at[pl.ds(owned + CAP * k, CAP)], sends[k], o_sem.at[k])
        for k in range(4)
    ]
    copies.append(pltpu.make_async_copy(obuf.at[pl.ds(0, owned)], own_out, o_sem.at[4]))
    for copy in copies:
        copy.start()
    for copy in copies:
        copy.wait()


def remap(fields, weights, source_block, target_block, owned, sectors):
    nb, width, _ = weights.shape
    cols = fields.shape[-1]
    groups_dev = target_block.shape[0]
    block = (width, cols)
    hbm = pl.BlockSpec(memory_space=pl.ANY)
    smem = pl.BlockSpec(memory_space=pltpu.SMEM)
    return pl.pallas_call(
        functools.partial(remap_kernel, sectors, owned, nb // groups_dev),
        out_shape=[jax.ShapeDtypeStruct((CAP, *block), jnp.bfloat16)] * 4
        + [jax.ShapeDtypeStruct((owned, *block), jnp.bfloat16)],
        in_specs=[smem, smem, hbm, hbm],
        out_specs=[hbm] * 5,
        scratch_shapes=[
            pltpu.VMEM(weights.shape, jnp.bfloat16),
            pltpu.VMEM(fields.shape, jnp.bfloat16),
            pltpu.VMEM((owned + 4 * CAP, *block), jnp.bfloat16),
            pltpu.SMEM((4,), jnp.int32),
            pltpu.SemaphoreType.DMA((groups_dev // CHUNK,)),
            pltpu.SemaphoreType.DMA,
            pltpu.SemaphoreType.DMA((5,)),
        ],
        compiler_params=pltpu.CompilerParams(vmem_limit_bytes=40 * 2**20),
        cost_estimate=pl.CostEstimate(
            flops=2 * nb * width * width * cols, bytes_accessed=19 * 2**20, transcendentals=0
        ),
        name="remap",
    )(source_block, target_block, weights, fields)


STEP = 8


def combine_kernel(slots, own, r0, r1, r2, r3, pool, ten, nine, eight):
    base = pl.program_id(0) * STEP
    received = (r0, r1, r2, r3)
    n9 = nine.shape[1]
    for j in range(STEP):
        total = own[j].astype(jnp.float32)
        for k in range(4):
            slot = slots[k, base + j]
            part = received[k][jnp.maximum(slot, 0)].astype(jnp.float32)
            total = total + jnp.where(slot >= 0, part, 0.0)
        rounded = total.astype(jnp.bfloat16)
        ten[j] = rounded
        means = jnp.dot(pool[j], rounded, preferred_element_type=jnp.float32)
        nine[j] = means[:n9]
        eight[j] = means[n9:]


def combine(slots, own, received, pool):
    owned, width, cols = own.shape
    n9, n8 = width // 4, width // 16
    whole = pl.BlockSpec(memory_space=pltpu.VMEM)

    def rows(n):
        return pl.BlockSpec((STEP, n, cols), lambda i: (i, 0, 0))

    return pl.pallas_call(
        combine_kernel,
        grid=(owned // STEP,),
        out_shape=[
            jax.ShapeDtypeStruct((owned, width, cols), jnp.bfloat16),
            jax.ShapeDtypeStruct((owned, n9, cols), jnp.float32),
            jax.ShapeDtypeStruct((owned, n8, cols), jnp.float32),
        ],
        in_specs=[pl.BlockSpec(memory_space=pltpu.SMEM), rows(width)]
        + [whole] * 4
        + [pl.BlockSpec((STEP, n9 + n8, width), lambda i: (i, 0, 0))],
        out_specs=[rows(width), rows(n9), rows(n8)],
        compiler_params=pltpu.CompilerParams(vmem_limit_bytes=24 * 2**20),
        cost_estimate=pl.CostEstimate(
            flops=2 * owned * 40 * width * cols, bytes_accessed=8 * 2**20, transcendentals=0
        ),
        name="combine",
    )(slots, own, *received, pool)


def pool_matrix(area, width):
    rows = area.reshape(-1, 1, width)
    pixel = jnp.arange(width)
    member = jnp.concatenate(
        [
            pixel[None, :] // 4 == jnp.arange(width // 4)[:, None],
            pixel[None, :] // 16 == jnp.arange(width // 16)[:, None],
        ],
        axis=0,
    )
    chosen = jnp.where(member[None], rows, 0.0)
    return (chosen / chosen.sum(2, keepdims=True)).astype(jnp.bfloat16)


def receive_slots(targets, me, owned):
    mine = targets // owned == me
    rank = jnp.cumsum(mine.astype(jnp.int32), axis=1)
    here = targets[:, None, :] == me * owned + jnp.arange(owned)[None, :, None]
    return jnp.sum(jnp.where(here, rank[:, None, :], 0), axis=2) - 1


def per_device(fields, weights, source_block, target_block, area):
    width = weights.shape[1]
    cols = fields.shape[1]
    owned = area.shape[0] // width
    sectors = lax.axis_size("sector")
    me = lax.axis_index("sector")
    targets = jnp.stack([shifted(target_block, "sector", move) for move in MOVES])
    outs = remap(
        fields.reshape(-1, width, cols), weights, source_block, target_block, owned, sectors
    )
    received = [shifted(outs[k], "sector", move) for k, move in enumerate(MOVES)]
    slots = receive_slots(targets, me, owned)
    pool = pool_matrix(area, width)
    ten, nine, eight = combine(slots, outs[4], received, pool)
    return ten.reshape(-1, cols), nine.reshape(-1, cols), eight.reshape(-1, cols)


def solution(mesh):
    in_specs = (
        P(("groups", "sector"), None),
        P("sector", None, None),
        P("sector"),
        P("sector"),
        P("sector"),
    )
    out_specs = (P(("groups", "sector"), None),) * 3
    return jax.shard_map(
        per_device, mesh=mesh, in_specs=in_specs, out_specs=out_specs, check_vma=False
    )
```

time: 170 us -> 62 us (0.36)
  waiting for transfers between devices: 84.4 us -> 27.6 us
  other arithmetic: 31.6 us -> 0.96 us
  local copies, waits for them, and re-layouts: 25.7 us -> 3.53 us
  matrix products: 21.7 us -> 0 us
  Pallas kernels: 0 us -> 14.3 us
  starting transfers between devices: 5.22 us -> 14.7 us
    ppermute x4 -> x8, waiting for transfers between devices: 84.4 us -> 27.6 us  [shifted(): return lax.ppermute(block, axis, route)]
    reduce_sum x5 -> x1, other arithmetic: 23.9 us -> 0.21 us  [receive_slots(): return jnp.sum(jnp.where(here, rank[:, None, :], 0), axis=2) - 1]
    dot_general x6 -> x0, matrix products: 21.7 us -> none  [the longest x1 15.5 us: per_device(): jnp.einsum('kps,ksc->kpc', weights, picked, preferred_element_type=jnp.fl...]
    pallas_call x0 -> x2, Pallas kernels: none -> 14.3 us  [the longest x1 8.21 us: remap(): pl.pallas_call(functools.partial(remap_kernel, sectors, owned, nb // grou...]
    gather x1 -> x0, local copies, waits for them, and re-layouts: 12.9 us -> none  [per_device(): picked = source_blocks[source_block]]
    ppermute x4 -> x8, starting transfers between devices: 5.22 us -> 14.7 us  [shifted(): return lax.ppermute(block, axis, route)]
    convert_element_type x2 -> x0, local copies, waits for them, and re-layouts: 8.01 us -> none  [the longest x1 4.26 us: per_device(): level10 = flat.astype(jnp.bfloat16)]
    convert_element_type x1, other arithmetic: 4.82 us -> 0.02 us  [receive_slots(): rank = jnp.cumsum(mine.astype(jnp.int32), axis=1)]
  transfers between devices with their start and end apart: 4 -> 8, of which waited for: 3 -> 4; matrix products, arithmetic and copies ran while one was open for 6% -> 2% of each run, Pallas kernels for 0% -> 13%
where the time goes in v1:
time: 62 us; the launch traced here: 61.8 us
  waiting for transfers between devices  27.6 us (45%)
  starting transfers between devices  14.7 us (24%)
  Pallas kernels  14.3 us (23%)
  local copies, waits for them, and re-layouts  3.53 us (6%)
  other arithmetic  0.96 us (2%)
  between operations  0.71 us (1%)
    ppermute x8, waiting for transfers between devices, shifted(): return lax.ppermute(block, axis, route)  27.6 us
    ppermute x8, starting transfers between devices, shifted(): return lax.ppermute(block, axis, route)  14.7 us
    pallas_call x1, Pallas kernels, remap(): pl.pallas_call(functools.partial(remap_kernel, sectors, owned, nb // grou...  8.21 us
    pallas_call x1, Pallas kernels, combine(): pl.pallas_call(combine_kernel, grid=(owned // STEP,), out_shape=[jax.Shap...  6.05 us
    unnamed x8, local copies, waits for them, and re-layouts  3.53 us
  transfers between devices with their start and end apart: 8, of which 4 were waited for; matrix products, arithmetic and copies ran while one was open for 2% of the time, Pallas kernels for 13%

profile of v1, /device:TPU:1, one launch (start us, length us, event | category | flops | bytes accessed | tf_op | source)
XLA Modules:
  0.0 61.8 jit_solution(13535535995667756272)
XLA Ops:
  0.6 2.7 %collective-permute-start.2 = (s32[80]{0:T(128)}, s32[80]{0:T(128)S(1)}, u32[]{:S(2)}, u32[]{:S(2)}) collective-permute-start(s32[80]{0:T(128)} %target.1), channel_id=1, source_target_pairs={{15,0},{0,1},{1,2},{2,3},{3,4},{4,5},{5,6},{6,7},{7,8},{8,9},{9,10... | collective-permute-start | bytes 968 | tf_op jit(solution)/shard_map/ppermute | solution.py:18
  3.3 2.5 %collective-permute-start.1 = (s32[80]{0:T(128)}, s32[80]{0:T(128)S(1)}, u32[]{:S(2)}, u32[]{:S(2)}) collective-permute-start(s32[80]{0:T(128)} %target.1), channel_id=1, source_target_pairs={{2,0},{3,1},{4,2},{5,3},{6,4},{7,5},{8,6},{9,7},{10,8},{11,9},{12,... | collective-permute-start | bytes 968 | tf_op jit(solution)/shard_map/ppermute | solution.py:18
  5.9 0.0 collective-permute-start
  5.9 1.0 %collective-permute-start.3 = (s32[80]{0:T(128)}, s32[80]{0:T(128)S(1)}, u32[]{:S(2)}, u32[]{:S(2)}) collective-permute-start(s32[80]{0:T(128)} %target.1), channel_id=1, source_target_pairs={{1,0},{2,1},{3,2},{4,3},{5,4},{6,5},{7,6},{8,7},{9,8},{10,9},{11,1... | collective-permute-start | bytes 968 | tf_op jit(solution)/shard_map/ppermute | solution.py:18
  6.8 0.0 copy-start
  6.8 2.2 %copy-done = bf16[16384,128]{1,0:T(8,128)(2,1)S(1)} copy-done((bf16[16384,128]{1,0:T(8,128)(2,1)S(1)}, bf16[16384,128]{1,0:T(8,128)(2,1)}, u32[]{:S(2)}) %copy-start) | copy-done | bytes 4194328
  9.0 0.0 copy-start.1
  9.0 0.7 %copy-done.1 = s32[320]{0:T(512)S(1)} copy-done((s32[320]{0:T(512)S(1)}, s32[320]{0:T(512)}, u32[]{:S(2)}) %copy-start.1) | copy-done | bytes 1304
  9.7 0.0 copy-start.2
  9.7 0.7 %copy-done.2 = s32[80]{0:T(128)S(1)} copy-done((s32[80]{0:T(128)S(1)}, s32[80]{0:T(128)}, u32[]{:S(2)}) %copy-start.2) | copy-done | bytes 344
  10.3 0.0 copy-start.3
  10.3 8.2 %remap.1 = (bf16[16,128,128]{2,1,0:T(8,128)(2,1)}, bf16[16,128,128]{2,1,0:T(8,128)(2,1)}, bf16[16,128,128]{2,1,0:T(8,128)(2,1)}, bf16[16,128,128]{2,1,0:T(8,128)(2,1)}, bf16[64,128,128]{2,1,0:T(8,128)(2,1)S(1)}) custom-call(s32[320]{0:T(512)S(1)} %copy-done.1, s32[80]{0:T(128)S(1)} %copy-done.2, bf16[320,128,128]{2,1,0:T(8,128)(2,1)} %w_hbm.1, ...), custom_call_target="tpu_custom_call" | custom-call | flops 1342177280 | bytes 19922944 | tf_op jit(solution)/shard_map/remap/pallas_call | solution.py:88
  18.6 0.2 collective-permute-start.4
  18.8 0.0 copy-done.3
  18.8 0.4 fusion.4.pool
  19.2 0.0 collective-permute-done.2
  19.2 4.4 %collective-permute-start.5 = (bf16[16,128,128]{2,1,0:T(8,128)(2,1)}, bf16[16,128,128]{2,1,0:T(8,128)(2,1)}, u32[]{:S(2)}, u32[]{:S(2)}) collective-permute-start(bf16[16,128,128]{2,1,0:T(8,128)(2,1)} %get-tuple-element.13), channel_id=1, source_target_pairs={{2,0},{3,1},{4,2},{5,3},{6,4},{7,5},{8,6},{9,7},{10,8},{11,9},{12,... | collective-permute-start | bytes 1572872 | tf_op jit(solution)/shard_map/ppermute | solution.py:18
  23.6 0.0 collective-permute-done.1
  23.7 0.8 %collective-permute-start.6 = (bf16[16,128,128]{2,1,0:T(8,128)(2,1)}, bf16[16,128,128]{2,1,0:T(8,128)(2,1)}, u32[]{:S(2)}, u32[]{:S(2)}) collective-permute-start(bf16[16,128,128]{2,1,0:T(8,128)(2,1)} %get-tuple-element.14), channel_id=1, source_target_pairs={{15,0},{0,1},{1,2},{2,3},{3,4},{4,5},{5,6},{6,7},{7,8},{8,9},{9,10... | collective-permute-start | bytes 1572872 | tf_op jit(solution)/shard_map/ppermute | solution.py:18
  24.4 0.0 collective-permute-done
  24.4 3.1 %collective-permute-start.7 = (bf16[16,128,128]{2,1,0:T(8,128)(2,1)}, bf16[16,128,128]{2,1,0:T(8,128)(2,1)}, u32[]{:S(2)}, u32[]{:S(2)}) collective-permute-start(bf16[16,128,128]{2,1,0:T(8,128)(2,1)} %get-tuple-element.15), channel_id=1, source_target_pairs={{1,0},{2,1},{3,2},{4,3},{5,4},{6,5},{7,6},{8,7},{9,8},{10,9},{11,1... | collective-permute-start | bytes 1572872 | tf_op jit(solution)/shard_map/ppermute | solution.py:18
  27.6 0.0 collective-permute-done.3
  27.6 0.3 reduce_window_sum.11
  27.9 0.2 select_reduce_fusion.1
  28.1 17.6 %collective-permute-done.4.r0 = bf16[16,128,128]{2,1,0:T(8,128)(2,1)S(1)} collective-permute-done((bf16[16,128,128]{2,1,0:T(8,128)(2,1)}, bf16[16,128,128]{2,1,0:T(8,128)(2,1)S(1)}, u32[]{:S(2)}, u32[]{:S(2)}) %collective-permute-start.4) | collective-permute-done | bytes 524320 | tf_op jit(solution)/shard_map/ppermute | solution.py:18
  45.7 2.2 %collective-permute-done.5.r1 = bf16[16,128,128]{2,1,0:T(8,128)(2,1)} collective-permute-done((bf16[16,128,128]{2,1,0:T(8,128)(2,1)}, bf16[16,128,128]{2,1,0:T(8,128)(2,1)}, u32[]{:S(2)}, u32[]{:S(2)}) %collective-permute-start.5) | collective-permute-done | bytes 524320 | tf_op jit(solution)/shard_map/ppermute | solution.py:18
  47.9 5.3 %collective-permute-done.6.r2 = bf16[16,128,128]{2,1,0:T(8,128)(2,1)} collective-permute-done((bf16[16,128,128]{2,1,0:T(8,128)(2,1)}, bf16[16,128,128]{2,1,0:T(8,128)(2,1)}, u32[]{:S(2)}, u32[]{:S(2)}) %collective-permute-start.6) | collective-permute-done | bytes 524320 | tf_op jit(solution)/shard_map/ppermute | solution.py:18
  53.3 2.5 %collective-permute-done.7.r3 = bf16[16,128,128]{2,1,0:T(8,128)(2,1)} collective-permute-done((bf16[16,128,128]{2,1,0:T(8,128)(2,1)}, bf16[16,128,128]{2,1,0:T(8,128)(2,1)}, u32[]{:S(2)}, u32[]{:S(2)}) %collective-permute-start.7) | collective-permute-done | bytes 524320 | tf_op jit(solution)/shard_map/ppermute | solution.py:18
  55.7 6.0 %combine.1 = (bf16[64,128,128]{2,1,0:T(8,128)(2,1)}, f32[64,32,128]{2,1,0:T(8,128)}, f32[64,8,128]{2,1,0:T(8,128)}) custom-call(s32[4,64]{1,0:T(4,128)S(1)} %broadcast_add_fusion.slots, bf16[64,128,128]{2,1,0:T(8,128)(2,1)S(1)} %get-tuple-element.11.own, bf16[16,128,128]{2,1,0:T(8,128)(2,1)S(1)} %collective-permute-done.4.r0, ...), custom_call_target="tpu_custom_call" | custom-call | flops 83886080 | bytes 8388608 | tf_op jit(solution)/shard_map/combine/pallas_call | solution.py:139
  (9 shorter events, 0.1 us)
Async XLA Ops:
  0.6 18.6 %collective-permute-start.2 = (s32[80]{0:T(128)}, s32[80]{0:T(128)S(1)}, u32[]{:S(2)}, u32[]{:S(2)}) collective-permute-start(s32[80]{0:T(128)} %target.1), channel_id=1, source_target_pairs={{15,0},{0,1},{1,2},{2,3},{3,4},{4,5},{5,6},{6,7},{7,8},{8,9},{9,10... | collective-permute-start | bytes 968 | tf_op jit(solution)/shard_map/ppermute | solution.py:18
  3.3 20.3 %collective-permute-start.1 = (s32[80]{0:T(128)}, s32[80]{0:T(128)S(1)}, u32[]{:S(2)}, u32[]{:S(2)}) collective-permute-start(s32[80]{0:T(128)} %target.1), channel_id=1, source_target_pairs={{2,0},{3,1},{4,2},{5,3},{6,4},{7,5},{8,6},{9,7},{10,8},{11,9},{12,... | collective-permute-start | bytes 968 | tf_op jit(solution)/shard_map/ppermute | solution.py:18
  5.9 18.6 %collective-permute-start = (s32[80]{0:T(128)}, s32[80]{0:T(128)S(1)}, u32[]{:S(2)}, u32[]{:S(2)}) collective-permute-start(s32[80]{0:T(128)} %target.1), channel_id=1, source_target_pairs={{14,0},{15,1},{0,2},{1,3},{2,4},{3,5},{4,6},{5,7},{6,8},{7,9},{8,1... | collective-permute-start | bytes 968 | tf_op jit(solution)/shard_map/ppermute | solution.py:18
  5.9 21.7 %collective-permute-start.3 = (s32[80]{0:T(128)}, s32[80]{0:T(128)S(1)}, u32[]{:S(2)}, u32[]{:S(2)}) collective-permute-start(s32[80]{0:T(128)} %target.1), channel_id=1, source_target_pairs={{1,0},{2,1},{3,2},{4,3},{5,4},{6,5},{7,6},{8,7},{9,8},{10,9},{11,1... | collective-permute-start | bytes 968 | tf_op jit(solution)/shard_map/ppermute | solution.py:18
  6.8 2.2 %copy-start = (bf16[16384,128]{1,0:T(8,128)(2,1)S(1)}, bf16[16384,128]{1,0:T(8,128)(2,1)}, u32[]{:S(2)}) copy-start(bf16[16384,128]{1,0:T(8,128)(2,1)} %param.5) | copy-start | bytes 12582916
  9.0 0.7 %copy-start.1 = (s32[320]{0:T(512)S(1)}, s32[320]{0:T(512)}, u32[]{:S(2)}) copy-start(s32[320]{0:T(512)} %source.1) | copy-start | bytes 3844
  9.7 0.7 %copy-start.2 = (s32[80]{0:T(128)S(1)}, s32[80]{0:T(128)}, u32[]{:S(2)}) copy-start(s32[80]{0:T(128)} %target.1) | copy-start | bytes 964
  10.3 8.4 %copy-start.3 = (f32[8192]{0:T(1024)S(1)}, f32[8192]{0:T(1024)}, u32[]{:S(2)}) copy-start(f32[8192]{0:T(1024)} %param.9) | copy-start | bytes 98308
  18.6 27.1 %collective-permute-start.4 = (bf16[16,128,128]{2,1,0:T(8,128)(2,1)}, bf16[16,128,128]{2,1,0:T(8,128)(2,1)S(1)}, u32[]{:S(2)}, u32[]{:S(2)}) collective-permute-start(bf16[16,128,128]{2,1,0:T(8,128)(2,1)} %get-tuple-element.12), channel_id=1, source_target_pairs={{14,0},{15,1},{0,2},{1,3},{2,4},{3,5},{4,6},{5,7},{6,8},{7,9},{8,1... | collective-permute-start | bytes 1572872 | tf_op jit(solution)/shard_map/ppermute | solution.py:18
  19.2 28.7 %collective-permute-start.5 = (bf16[16,128,128]{2,1,0:T(8,128)(2,1)}, bf16[16,128,128]{2,1,0:T(8,128)(2,1)}, u32[]{:S(2)}, u32[]{:S(2)}) collective-permute-start(bf16[16,128,128]{2,1,0:T(8,128)(2,1)} %get-tuple-element.13), channel_id=1, source_target_pairs={{2,0},{3,1},{4,2},{5,3},{6,4},{7,5},{8,6},{9,7},{10,8},{11,9},{12,... | collective-permute-start | bytes 1572872 | tf_op jit(solution)/shard_map/ppermute | solution.py:18
  23.7 29.6 %collective-permute-start.6 = (bf16[16,128,128]{2,1,0:T(8,128)(2,1)}, bf16[16,128,128]{2,1,0:T(8,128)(2,1)}, u32[]{:S(2)}, u32[]{:S(2)}) collective-permute-start(bf16[16,128,128]{2,1,0:T(8,128)(2,1)} %get-tuple-element.14), channel_id=1, source_target_pairs={{15,0},{0,1},{1,2},{2,3},{3,4},{4,5},{5,6},{6,7},{7,8},{8,9},{9,10... | collective-permute-start | bytes 1572872 | tf_op jit(solution)/shard_map/ppermute | solution.py:18
  24.4 31.3 %collective-permute-start.7 = (bf16[16,128,128]{2,1,0:T(8,128)(2,1)}, bf16[16,128,128]{2,1,0:T(8,128)(2,1)}, u32[]{:S(2)}, u32[]{:S(2)}) collective-permute-start(bf16[16,128,128]{2,1,0:T(8,128)(2,1)} %get-tuple-element.15), channel_id=1, source_target_pairs={{1,0},{2,1},{3,2},{4,3},{5,4},{6,5},{7,6},{8,7},{9,8},{10,9},{11,1... | collective-permute-start | bytes 1572872 | tf_op jit(solution)/shard_map/ppermute | solution.py:18

commit v2 on v1

v2 whole, which is shorter than its diff:
```python
import functools

import jax
import jax.numpy as jnp
from jax import lax
from jax.experimental import pallas as pl
from jax.experimental.pallas import tpu as pltpu
from jax.sharding import PartitionSpec as P

CAP = 16
MOVES = (2, -2, 1, -1)
CHUNK = 8
STEP = 8
HBM = pl.BlockSpec(memory_space=pl.ANY)


def product(wbuf, fbuf, source, w_first, s_first, per_group):
    left = jnp.concatenate([wbuf[w_first + q] for q in range(per_group)], axis=1)
    right = jnp.concatenate(
        [fbuf[source[s_first + q]] for q in range(per_group)], axis=0
    )
    value = jnp.dot(left, right, preferred_element_type=jnp.float32)
    return value.astype(jnp.bfloat16)


def field_copies(f_hbm, fbuf, f_sem, parts):
    rows = fbuf.shape[0] // parts
    return [
        pltpu.make_async_copy(
            f_hbm.at[pl.ds(i * rows, rows)], fbuf.at[pl.ds(i * rows, rows)], f_sem.at[i]
        )
        for i in range(parts)
    ]


def outgoing_kernel(sectors, owned, per_group, source_hbm, target_hbm, w_hbm, f_hbm, *rest):
    sends, tables_out = rest[:4], rest[4:9]
    source, target = rest[9:11]
    tables = rest[11:16]
    wbuf, fbuf, obuf, count, chosen, i_sem, w_sem, f_sem, o_sem = rest[16:]
    groups_dev = target.shape[0]
    index_copies = [
        pltpu.make_async_copy(target_hbm, target, i_sem.at[0]),
        pltpu.make_async_copy(source_hbm, source, i_sem.at[1]),
    ]
    for copy in index_copies:
        copy.start()
    fields_in = field_copies(f_hbm, fbuf, f_sem, f_sem.shape[0])
    for copy in fields_in:
        copy.start()
    me = lax.axis_index("sector")
    for k in range(5):
        count[k] = 0

    @pl.loop(0, owned, unroll=8)
    def _(t):
        for table in tables:
            table[t] = -1

    def w_copy(g, slot):
        return pltpu.make_async_copy(
            w_hbm.at[pl.ds(g * per_group, per_group)],
            wbuf.at[pl.ds(slot * per_group, per_group)],
            w_sem.at[slot],
        )

    for copy in index_copies:
        copy.wait()

    for k, move in enumerate(MOVES):
        owner = lax.rem(me + sectors + move, sectors)
        first = owner * owned

        @pl.loop(0, groups_dev, unroll=4)
        def _(g):
            local = target[g] - first

            @pl.when((local >= 0) & (local < owned))
            def _():
                rank = count[k]
                count[k] = rank + 1
                chosen[k * CAP + rank] = g
                tables[k][local] = rank
                w_copy(g, k * CAP + rank).start()

    @pl.loop(0, groups_dev, unroll=4)
    def _(g):
        local = target[g] - me * owned

        @pl.when((local >= 0) & (local < owned))
        def _():
            tables[4][local] = g

    table_copies = [
        pltpu.make_async_copy(tables[k], tables_out[k], o_sem.at[4 + k]) for k in range(5)
    ]
    for copy in table_copies:
        copy.start()
    for copy in fields_in:
        copy.wait()

    copies = []
    for k in range(4):

        @pl.loop(0, count[k])
        def _(rank):
            slot = k * CAP + rank
            g = chosen[slot]
            w_copy(g, slot).wait()
            obuf[slot] = product(
                wbuf, fbuf, source, slot * per_group, g * per_group, per_group
            )

        copies.append(
            pltpu.make_async_copy(obuf.at[pl.ds(CAP * k, CAP)], sends[k], o_sem.at[k])
        )
        copies[-1].start()
    for copy in copies + table_copies:
        copy.wait()


def outgoing(fields, weights, source_block, target_block, owned, sectors):
    nb, width, _ = weights.shape
    cols = fields.shape[-1]
    groups_dev = target_block.shape[0]
    per_group = nb // groups_dev
    block = (width, cols)
    table = -(-owned // 128) * 128
    return pl.pallas_call(
        functools.partial(outgoing_kernel, sectors, owned, per_group),
        out_shape=[jax.ShapeDtypeStruct((CAP, *block), jnp.bfloat16)] * 4
        + [jax.ShapeDtypeStruct((table,), jnp.int32)] * 5,
        in_specs=[HBM] * 4,
        out_specs=[HBM] * 9,
        scratch_shapes=[pltpu.SMEM((nb,), jnp.int32), pltpu.SMEM((groups_dev,), jnp.int32)]
        + [pltpu.SMEM((table,), jnp.int32)] * 5
        + [
            pltpu.VMEM((4 * CAP * per_group, width, width), jnp.bfloat16),
            pltpu.VMEM(fields.shape, jnp.bfloat16),
            pltpu.VMEM((4 * CAP, *block), jnp.bfloat16),
            pltpu.SMEM((5,), jnp.int32),
            pltpu.SMEM((4 * CAP,), jnp.int32),
            pltpu.SemaphoreType.DMA((2,)),
            pltpu.SemaphoreType.DMA((4 * CAP,)),
            pltpu.SemaphoreType.DMA((4,)),
            pltpu.SemaphoreType.DMA((9,)),
        ],
        compiler_params=pltpu.CompilerParams(vmem_limit_bytes=60 * 2**20),
        name="outgoing",
    )(source_block, target_block, weights, fields)


def exchange_kernel(per_group, sectors, *refs):
    sends, tables = refs[:4], refs[4:8]
    own_table_hbm, source_hbm, w_hbm, f_hbm, area = refs[8:13]
    received, tables_out, own_out, pool = refs[13:17], refs[17:21], refs[21], refs[22]
    own_table, source, wbuf, fbuf, pbuf, obuf = refs[23:29]
    send_sem, recv_sem, i_sem, w_sem, f_sem, o_sem = refs[29:]
    me = lax.axis_index("sector")
    chunks = w_sem.shape[0]
    per_chunk = CHUNK * per_group
    owned = obuf.shape[0]
    barrier = pltpu.get_barrier_semaphore()
    for move in MOVES:
        pl.semaphore_signal(
            barrier,
            inc=1,
            device_id={"sector": lax.rem(me + sectors + move, sectors)},
            device_id_type=pl.DeviceIdType.MESH,
        )
    pl.semaphore_wait(barrier, len(MOVES))
    remote = []
    for k, move in enumerate(MOVES):
        peer = {"sector": lax.rem(me + sectors + move, sectors)}
        for index, source_ref, target_ref in (
            (k, sends[k], received[k]),
            (4 + k, tables[k], tables_out[k]),
        ):
            remote.append(
                pltpu.make_async_remote_copy(
                    src_ref=source_ref,
                    dst_ref=target_ref,
                    send_sem=send_sem.at[index],
                    recv_sem=recv_sem.at[index],
                    device_id=peer,
                    device_id_type=pl.DeviceIdType.MESH,
                )
            )
            remote[-1].start()
    index_copies = [
        pltpu.make_async_copy(own_table_hbm, own_table, i_sem.at[0]),
        pltpu.make_async_copy(source_hbm, source, i_sem.at[1]),
    ]
    local = index_copies + field_copies(f_hbm, fbuf, f_sem, f_sem.shape[0])
    for copy in local:
        copy.start()

    def w_copy(c):
        rows = pl.ds(c * per_chunk, per_chunk)
        return pltpu.make_async_copy(w_hbm.at[rows], wbuf.at[rows], w_sem.at[c])

    for c in range(chunks):
        w_copy(c).start()
    width = area.shape[1]
    rows = pool.shape[1]
    n9 = width // 4
    row = lax.broadcasted_iota(jnp.int32, (rows, width), 0)
    pixel = lax.broadcasted_iota(jnp.int32, (rows, width), 1)
    member = jnp.where(row < n9, pixel // 4 - row, pixel // 16 - (row - n9)) == 0

    @pl.loop(0, owned)
    def _(t):
        share = jnp.where(member, area[pl.ds(t, 1), :], 0.0)
        pool[t] = (share / share.sum(1, keepdims=True)).astype(pool.dtype)

    for copy in local:
        copy.wait()

    @pl.loop(0, chunks)
    def _(c):
        w_copy(c).wait()

        @pl.loop(0, CHUNK)
        def _(p):
            g = c * CHUNK + p
            pbuf[g] = product(wbuf, fbuf, source, g * per_group, g * per_group, per_group)

    @pl.loop(0, owned)
    def _(t):
        g = own_table[t]
        value = pbuf[jnp.maximum(g, 0)]
        obuf[t] = jnp.where(g >= 0, value.astype(jnp.float32), 0.0).astype(obuf.dtype)

    out = pltpu.make_async_copy(obuf, own_out, o_sem)
    out.start()
    out.wait()
    for copy in remote:
        copy.wait()


def exchange(sends, tables, fields, weights, source_block, area, sectors, groups_dev):
    nb, width, _ = weights.shape
    cols = fields.shape[-1]
    owned = area.shape[0]
    block = (width, cols)
    vmem = pl.BlockSpec(memory_space=pltpu.VMEM)
    table = jax.ShapeDtypeStruct(tables[0].shape, jnp.int32)
    return pl.pallas_call(
        functools.partial(exchange_kernel, nb // groups_dev, sectors),
        out_shape=[jax.ShapeDtypeStruct((CAP, *block), jnp.bfloat16)] * 4
        + [table] * 4
        + [
            jax.ShapeDtypeStruct((owned, *block), jnp.bfloat16),
            jax.ShapeDtypeStruct((owned, width // 4 + width // 16, width), jnp.bfloat16),
        ],
        in_specs=[HBM] * 12 + [vmem],
        out_specs=[HBM] * 9 + [vmem],
        scratch_shapes=[
            pltpu.SMEM(tables[4].shape, jnp.int32),
            pltpu.SMEM((nb,), jnp.int32),
            pltpu.VMEM(weights.shape, jnp.bfloat16),
            pltpu.VMEM(fields.shape, jnp.bfloat16),
            pltpu.VMEM((groups_dev, *block), jnp.bfloat16),
            pltpu.VMEM((owned, *block), jnp.bfloat16),
            pltpu.SemaphoreType.DMA((8,)),
            pltpu.SemaphoreType.DMA((8,)),
            pltpu.SemaphoreType.DMA((2,)),
            pltpu.SemaphoreType.DMA((groups_dev // CHUNK,)),
            pltpu.SemaphoreType.DMA((4,)),
            pltpu.SemaphoreType.DMA,
        ],
        compiler_params=pltpu.CompilerParams(
            collective_id=0, has_side_effects=True, vmem_limit_bytes=60 * 2**20
        ),
        name="exchange",
    )(*sends, *tables, source_block, weights, fields, area)


def combine_kernel(t0, t1, t2, t3, own, r0, r1, r2, r3, pool, ten, nine, eight, *scratch):
    slots, sem = scratch[:4], scratch[4]
    received = (r0, r1, r2, r3)

    @pl.when(pl.program_id(0) == 0)
    def _():
        copies = [
            pltpu.make_async_copy(table, slots[k], sem.at[k])
            for k, table in enumerate((t0, t1, t2, t3))
        ]
        for copy in copies:
            copy.start()
        for copy in copies:
            copy.wait()

    base = pl.program_id(0) * STEP
    n9 = nine.shape[1]
    for j in range(STEP):
        total = own[j].astype(jnp.float32)
        for k in range(4):
            slot = slots[k][base + j]
            part = received[k][jnp.maximum(slot, 0)].astype(jnp.float32)
            total = total + jnp.where(slot >= 0, part, 0.0)
        rounded = total.astype(jnp.bfloat16)
        ten[j] = rounded
        means = jnp.dot(pool[j], rounded, preferred_element_type=jnp.float32)
        nine[j] = means[:n9]
        eight[j] = means[n9:]


def combine(tables, own, received, pool):
    owned, width, cols = own.shape
    n9, n8 = width // 4, width // 16
    whole = pl.BlockSpec(memory_space=pltpu.VMEM)

    def rows(n):
        return pl.BlockSpec((STEP, n, cols), lambda i: (i, 0, 0))

    return pl.pallas_call(
        combine_kernel,
        grid=(owned // STEP,),
        out_shape=[
            jax.ShapeDtypeStruct((owned, width, cols), jnp.bfloat16),
            jax.ShapeDtypeStruct((owned, n9, cols), jnp.float32),
            jax.ShapeDtypeStruct((owned, n8, cols), jnp.float32),
        ],
        in_specs=[HBM] * 4
        + [rows(width)]
        + [whole] * 4
        + [pl.BlockSpec((STEP, n9 + n8, width), lambda i: (i, 0, 0))],
        out_specs=[rows(width), rows(n9), rows(n8)],
        scratch_shapes=[pltpu.SMEM(tables[0].shape, jnp.int32)] * 4
        + [pltpu.SemaphoreType.DMA((4,))],
        compiler_params=pltpu.CompilerParams(vmem_limit_bytes=60 * 2**20),
        name="combine",
    )(*tables, own, *received, pool)


def per_device(fields, weights, source_block, target_block, area):
    width = weights.shape[1]
    cols = fields.shape[1]
    owned = area.shape[0] // width
    sectors = lax.axis_size("sector")
    groups_dev = target_block.shape[0]
    blocks = fields.reshape(-1, width, cols)
    sent = outgoing(blocks, weights, source_block, target_block, owned, sectors)
    arrived = exchange(
        sent[:4], sent[4:], blocks, weights, source_block, area.reshape(owned, width), sectors,
        groups_dev,
    )
    ten, nine, eight = combine(arrived[4:8], arrived[8], arrived[:4], arrived[9])
    return ten.reshape(-1, cols), nine.reshape(-1, cols), eight.reshape(-1, cols)


def solution(mesh):
    in_specs = (
        P(("groups", "sector"), None),
        P("sector", None, None),
        P("sector"),
        P("sector"),
        P("sector"),
    )
    out_specs = (P(("groups", "sector"), None),) * 3
    return jax.shard_map(
        per_device, mesh=mesh, in_specs=in_specs, out_specs=out_specs, check_vma=False
    )
```

time: 62 us -> 64.2 us (1.035)
  Pallas kernels: 14.3 us -> 63 us
  waiting for transfers between devices: 27.6 us -> 0 us
  starting transfers between devices: 14.7 us -> 0 us
  local copies, waits for them, and re-layouts: 3.53 us -> 0 us
  other arithmetic: 0.96 us -> 0 us
    pallas_call x1 -> x2, Pallas kernels: 8.21 us -> 54.5 us  [the longest x1 42.7 us: exchange(): pl.pallas_call(functools.partial(exchange_kernel, nb // groups_dev, secto...]
    ppermute x8 -> x0, waiting for transfers between devices: 27.6 us -> none  [shifted(): return lax.ppermute(block, axis, route)]
    ppermute x8 -> x0, starting transfers between devices: 14.7 us -> none  [shifted(): return lax.ppermute(block, axis, route)]
    unnamed x8 -> x0, local copies, waits for them, and re-layouts: 3.53 us -> none
    pallas_call x1, Pallas kernels: 6.05 us -> 8.44 us  [combine(): pl.pallas_call(combine_kernel, grid=(owned // STEP,), out_shape=[jax.Shap...]
  transfers between devices with their start and end apart: 8 -> 0, of which waited for: 4 -> 0; matrix products, arithmetic and copies ran while one was open for 2% -> 0% of each run, Pallas kernels for 13% -> 0%
where the time goes in v2:
time: 64.2 us; the launch traced here: 63.6 us
  Pallas kernels  63 us (98%)
  between operations  0.65 us (1%)
    pallas_call x1, Pallas kernels, exchange(): pl.pallas_call(functools.partial(exchange_kernel, nb // groups_dev, secto...  42.7 us
    pallas_call x1, Pallas kernels, outgoing(): pl.pallas_call(functools.partial(outgoing_kernel, sectors, owned, per_gro...  11.9 us
    pallas_call x1, Pallas kernels, combine(): pl.pallas_call(combine_kernel, grid=(owned // STEP,), out_shape=[jax.Shap...  8.44 us

profile of v2, /device:TPU:1, one launch (start us, length us, event | category | flops | bytes accessed | tf_op | source)
XLA Modules:
  0.0 63.6 jit_solution(507609219731904210)
XLA Ops:
  0.6 11.9 %outgoing.1 = (bf16[16,128,128]{2,1,0:T(8,128)(2,1)}, bf16[16,128,128]{2,1,0:T(8,128)(2,1)}, bf16[16,128,128]{2,1,0:T(8,128)(2,1)}, bf16[16,128,128]{2,1,0:T(8,1...) custom-call(s32[320]{0:T(512)} %refs_9_.1, s32[80]{0:T(128)} %target_hbm.1, ...), custom_call_target="tpu_custom_call" | custom-call | tf_op jit(solution)/shard_map/outgoing/pallas_call | solution.py:129
  12.5 42.7 %exchange.1 = (bf16[16,128,128]{2,1,0:T(8,128)(2,1)}, bf16[16,128,128]{2,1,0:T(8,128)(2,1)}, bf16[16,128,128]{2,1,0:T(8,128)(2,1)}, bf16[16,128,128]{2,1,0:T(8,1...) custom-call(bf16[16,128,128]{2,1,0:T(8,128)(2,1)} %get-tuple-element, ...), custom_call_target="tpu_custom_call" | custom-call | tf_op jit(solution)/shard_map/exchange/pallas_call | solution.py:248
  55.2 8.4 %combine.1 = (bf16[64,128,128]{2,1,0:T(8,128)(2,1)}, f32[64,32,128]{2,1,0:T(8,128)}, f32[64,8,128]{2,1,0:T(8,128)}) custom-call(s32[128]{0:T(128)} %get-tuple-element.34.t0, s32[128]{0:T(128)} %get-tuple-element.35.t1, s32[128]{0:T(128)} %get-tuple-element.36.t2, s32[128]{0:T(128)} %get-tuple-element.37.t3, bf16[64,128,128]{2,1,0:T(8,128)(2,1)} %get-tuple-element.38.own, ...), custom_call_target="tpu_custom_call" | custom-call | tf_op jit(solution)/shard_map/combine/pallas_call | solution.py:317

commit v3 on v2

v3 whole, which is shorter than its diff:
```python
import functools

import jax
import jax.numpy as jnp
from jax import lax
from jax.experimental import pallas as pl
from jax.experimental.pallas import tpu as pltpu
from jax.sharding import PartitionSpec as P

CAP = 16
MOVES = (2, -2, 1, -1)
CHUNK = 8
STEP = 8
FIRST = 2
LANES = 128
HBM = pl.BlockSpec(memory_space=pl.ANY)


def product(wbuf, fbuf, source, w_first, s_first, per_group):
    left = jnp.concatenate([wbuf[w_first + q] for q in range(per_group)], axis=1)
    right = jnp.concatenate(
        [fbuf[source[s_first + q]] for q in range(per_group)], axis=0
    )
    value = jnp.dot(left, right, preferred_element_type=jnp.float32)
    return value.astype(jnp.bfloat16)


def field_copies(f_hbm, fbuf, f_sem, parts):
    rows = fbuf.shape[0] // parts
    return [
        pltpu.make_async_copy(
            f_hbm.at[pl.ds(i * rows, rows)], fbuf.at[pl.ds(i * rows, rows)], f_sem.at[i]
        )
        for i in range(parts)
    ]


def table_size(owned):
    width = -(-owned // LANES) * LANES
    return width, (len(MOVES) + 1) * width, -(-(len(MOVES) * CAP + 1) // LANES) * LANES


def outgoing_kernel(sectors, owned, per_group, source_hbm, target_hbm, w_hbm, f_hbm, *rest):
    sends, table_out = rest[:FIRST], rest[FIRST]
    source, target, table, wbuf, fbuf, obuf, count, i_sem, w_sem, f_sem, o_sem = rest[FIRST + 1 :]
    groups_dev = target.shape[0]
    kinds = len(MOVES)
    width, chosen, _ = table_size(owned)
    index_copies = [
        pltpu.make_async_copy(target_hbm, target, i_sem.at[0]),
        pltpu.make_async_copy(source_hbm, source, i_sem.at[1]),
    ]
    for copy in index_copies:
        copy.start()
    fields_in = field_copies(f_hbm, fbuf, f_sem, f_sem.shape[0])
    for copy in fields_in:
        copy.start()
    me = lax.axis_index("sector")
    for k in range(kinds + 1):
        count[k] = 0

    @pl.loop(0, owned, unroll=8)
    def _(t):
        for k in range(kinds + 1):
            table[k * width + t] = -1

    @pl.loop(0, kinds * CAP, unroll=8)
    def _(t):
        table[chosen + t] = 0

    def w_copy(g, slot):
        return pltpu.make_async_copy(
            w_hbm.at[pl.ds(g * per_group, per_group)],
            wbuf.at[pl.ds(slot * per_group, per_group)],
            w_sem.at[slot],
        )

    for copy in index_copies:
        copy.wait()

    @pl.loop(0, groups_dev, unroll=4)
    def _(g):
        where_to = target[g]
        owner = where_to // owned
        local = where_to - owner * owned
        distance = owner - me
        distance = jnp.where(distance < 0, distance + sectors, distance)
        kind = kinds
        for k, move in enumerate(MOVES):
            kind = jnp.where(distance == move % sectors, k, kind)
        rank = count[kind]
        count[kind] = rank + 1
        mine = kind == kinds
        slot = kind * CAP + jnp.where(mine, 0, rank)
        table[chosen + slot] = g
        table[kind * width + local] = jnp.where(mine, g, rank)

        @pl.when(kind < FIRST)
        def _():
            w_copy(g, slot).start()

    table_copy = pltpu.make_async_copy(table, table_out, o_sem.at[FIRST])
    table_copy.start()
    for copy in fields_in:
        copy.wait()

    unroll = 4
    copies = [table_copy]
    for k in range(FIRST):

        @pl.loop(0, (count[k] + unroll - 1) // unroll)
        def _(step):
            for r in range(unroll):
                rank = step * unroll + r
                slot = k * CAP + rank

                @pl.when(rank < count[k])
                def _():
                    w_copy(table[chosen + slot], slot).wait()

            for r in range(unroll):
                slot = k * CAP + step * unroll + r
                g = table[chosen + slot]
                obuf[slot] = product(
                    wbuf, fbuf, source, slot * per_group, g * per_group, per_group
                )

        copy = pltpu.make_async_copy(obuf.at[pl.ds(CAP * k, CAP)], sends[k], o_sem.at[k])
        copy.start()
        copies.append(copy)
    for copy in copies:
        copy.wait()


def outgoing(fields, weights, source_block, target_block, owned, sectors):
    nb, width, _ = weights.shape
    cols = fields.shape[-1]
    groups_dev = target_block.shape[0]
    per_group = nb // groups_dev
    block = (width, cols)
    _, chosen, tail = table_size(owned)
    return pl.pallas_call(
        functools.partial(outgoing_kernel, sectors, owned, per_group),
        out_shape=[jax.ShapeDtypeStruct((CAP, *block), jnp.bfloat16)] * FIRST
        + [jax.ShapeDtypeStruct((chosen + tail,), jnp.int32)],
        in_specs=[HBM] * 4,
        out_specs=[HBM] * (FIRST + 1),
        scratch_shapes=[
            pltpu.SMEM((nb,), jnp.int32),
            pltpu.SMEM((groups_dev,), jnp.int32),
            pltpu.SMEM((chosen + tail,), jnp.int32),
            pltpu.VMEM((FIRST * CAP * per_group, width, width), jnp.bfloat16),
            pltpu.VMEM(fields.shape, jnp.bfloat16),
            pltpu.VMEM((FIRST * CAP, *block), jnp.bfloat16),
            pltpu.SMEM((len(MOVES) + 1,), jnp.int32),
            pltpu.SemaphoreType.DMA((2,)),
            pltpu.SemaphoreType.DMA((FIRST * CAP,)),
            pltpu.SemaphoreType.DMA((4,)),
            pltpu.SemaphoreType.DMA((FIRST + 1,)),
        ],
        compiler_params=pltpu.CompilerParams(vmem_limit_bytes=60 * 2**20),
        name="outgoing",
    )(source_block, target_block, weights, fields)


def exchange_kernel(per_group, sectors, *refs):
    sends, table_hbm = refs[:FIRST], refs[FIRST]
    source_hbm, w_hbm, f_hbm, area = refs[FIRST + 1 : FIRST + 5]
    rest = refs[FIRST + 5 :]
    received, tables_out, own_out, pool = rest[:4], rest[4:8], rest[8], rest[9]
    table, source, wbuf, fbuf, pbuf, obuf, near0, near1 = rest[10:18]
    send_sem, recv_sem, i_sem, w_sem, f_sem, o_sem = rest[18:]
    near = (near0, near1)
    me = lax.axis_index("sector")
    kinds = len(MOVES)
    chunks = w_sem.shape[0]
    per_chunk = CHUNK * per_group
    owned = obuf.shape[0]
    own_row, chosen, _ = table_size(owned)
    own_row = kinds * own_row
    local = [
        pltpu.make_async_copy(table_hbm, table, i_sem.at[0]),
        pltpu.make_async_copy(source_hbm, source, i_sem.at[1]),
    ] + field_copies(f_hbm, fbuf, f_sem, f_sem.shape[0])
    peers = [{"sector": lax.rem(me + sectors + move, sectors)} for move in MOVES]
    barrier = pltpu.get_barrier_semaphore()
    for peer in peers:
        pl.semaphore_signal(
            barrier, inc=1, device_id=peer, device_id_type=pl.DeviceIdType.MESH
        )
    for copy in local:
        copy.start()

    def w_copy(c):
        rows = pl.ds(c * per_chunk, per_chunk)
        return pltpu.make_async_copy(w_hbm.at[rows], wbuf.at[rows], w_sem.at[c])

    pl.semaphore_wait(barrier, kinds)

    def remote(index, k, source_ref, target_ref):
        return pltpu.make_async_remote_copy(
            src_ref=source_ref,
            dst_ref=target_ref,
            send_sem=send_sem.at[index],
            recv_sem=recv_sem.at[index],
            device_id=peers[k],
            device_id_type=pl.DeviceIdType.MESH,
        )

    moved = [remote(k, k, sends[k], received[k]) for k in range(FIRST)]
    moved += [remote(kinds + k, k, table_hbm, tables_out[k]) for k in range(kinds)]
    for copy in moved:
        copy.start()
    for c in range(chunks):
        w_copy(c).start()
    for copy in local:
        copy.wait()

    @pl.loop(0, chunks)
    def _(c):
        w_copy(c).wait()

        @pl.loop(0, CHUNK // 4)
        def _(step):
            for p in range(4):
                g = c * CHUNK + step * 4 + p
                pbuf[g] = product(wbuf, fbuf, source, g * per_group, g * per_group, per_group)

    for k in range(FIRST, kinds):

        @pl.loop(0, CAP)
        def _(rank):
            near[k - FIRST][rank] = pbuf[table[chosen + k * CAP + rank]]

        moved.append(remote(k, k, near[k - FIRST], received[k]))
        moved[-1].start()

    @pl.loop(0, owned)
    def _(t):
        g = table[own_row + t]
        value = pbuf[jnp.maximum(g, 0)]
        obuf[t] = jnp.where(g >= 0, value.astype(jnp.float32), 0.0).astype(obuf.dtype)

    out = pltpu.make_async_copy(obuf, own_out, o_sem)
    out.start()
    width = area.shape[1]
    rows = pool.shape[1]
    n9 = width // 4
    row = lax.broadcasted_iota(jnp.int32, (rows, width), 0)
    pixel = lax.broadcasted_iota(jnp.int32, (rows, width), 1)
    member = jnp.where(row < n9, pixel // 4 - row, pixel // 16 - (row - n9)) == 0

    @pl.loop(0, owned)
    def _(t):
        share = jnp.where(member, area[pl.ds(t, 1), :], 0.0)
        pool[t] = (share / share.sum(1, keepdims=True)).astype(pool.dtype)

    out.wait()
    for copy in moved:
        copy.wait()


def exchange(sends, table, fields, weights, source_block, area, sectors, groups_dev):
    nb, width, _ = weights.shape
    cols = fields.shape[-1]
    owned = area.shape[0]
    block = (width, cols)
    vmem = pl.BlockSpec(memory_space=pltpu.VMEM)
    kinds = len(MOVES)
    return pl.pallas_call(
        functools.partial(exchange_kernel, nb // groups_dev, sectors),
        out_shape=[jax.ShapeDtypeStruct((CAP, *block), jnp.bfloat16)] * kinds
        + [jax.ShapeDtypeStruct(table.shape, jnp.int32)] * kinds
        + [
            jax.ShapeDtypeStruct((owned, *block), jnp.bfloat16),
            jax.ShapeDtypeStruct((owned, width // 4 + width // 16, width), jnp.bfloat16),
        ],
        in_specs=[HBM] * (FIRST + 4) + [vmem],
        out_specs=[HBM] * (2 * kinds + 1) + [vmem],
        scratch_shapes=[
            pltpu.SMEM(table.shape, jnp.int32),
            pltpu.SMEM((nb,), jnp.int32),
            pltpu.VMEM(weights.shape, jnp.bfloat16),
            pltpu.VMEM(fields.shape, jnp.bfloat16),
            pltpu.VMEM((groups_dev, *block), jnp.bfloat16),
            pltpu.VMEM((owned, *block), jnp.bfloat16),
            pltpu.VMEM((CAP, *block), jnp.bfloat16),
            pltpu.VMEM((CAP, *block), jnp.bfloat16),
            pltpu.SemaphoreType.DMA((2 * kinds,)),
            pltpu.SemaphoreType.DMA((2 * kinds,)),
            pltpu.SemaphoreType.DMA((2,)),
            pltpu.SemaphoreType.DMA((groups_dev // CHUNK,)),
            pltpu.SemaphoreType.DMA((4,)),
            pltpu.SemaphoreType.DMA,
        ],
        compiler_params=pltpu.CompilerParams(
            collective_id=0, has_side_effects=True, vmem_limit_bytes=60 * 2**20
        ),
        name="exchange",
    )(*sends, table, source_block, weights, fields, area)


def combine_kernel(row, *refs):
    tables, received_hbm, own, pool = refs[:4], refs[4:8], refs[8], refs[9]
    ten, nine, eight = refs[10:13]
    slots, received, acc, sem = refs[13:17], refs[17:21], refs[21], refs[22]

    @pl.when(pl.program_id(0) == 0)
    def _():
        copies = [
            pltpu.make_async_copy(table, slots[k], sem.at[k]) for k, table in enumerate(tables)
        ] + [
            pltpu.make_async_copy(part, received[k], sem.at[4 + k])
            for k, part in enumerate(received_hbm)
        ]
        for copy in copies:
            copy.start()
        for copy in copies:
            copy.wait()

    base = pl.program_id(0) * STEP
    n9 = nine.shape[1]
    for j in range(STEP):
        acc[j] = own[j].astype(jnp.float32)
    for j in range(STEP):
        for k in range(4):
            slot = slots[k][k * row + base + j]

            @pl.when(slot >= 0)
            def _():
                acc[j] += received[k][slot].astype(jnp.float32)

    for j in range(STEP):
        rounded = acc[j].astype(jnp.bfloat16)
        ten[j] = rounded
        means = jnp.dot(pool[j], rounded, preferred_element_type=jnp.float32)
        nine[j] = means[:n9]
        eight[j] = means[n9:]


def combine(tables, own, received, pool):
    owned, width, cols = own.shape
    n9, n8 = width // 4, width // 16

    def rows(n):
        return pl.BlockSpec((STEP, n, cols), lambda i: (i, 0, 0))

    return pl.pallas_call(
        functools.partial(combine_kernel, table_size(owned)[0]),
        grid=(owned // STEP,),
        out_shape=[
            jax.ShapeDtypeStruct((owned, width, cols), jnp.bfloat16),
            jax.ShapeDtypeStruct((owned, n9, cols), jnp.float32),
            jax.ShapeDtypeStruct((owned, n8, cols), jnp.float32),
        ],
        in_specs=[HBM] * 8
        + [rows(width)]
        + [pl.BlockSpec((STEP, n9 + n8, width), lambda i: (i, 0, 0))],
        out_specs=[rows(width), rows(n9), rows(n8)],
        scratch_shapes=[pltpu.SMEM(tables[0].shape, jnp.int32)] * 4
        + [pltpu.VMEM(received[0].shape, jnp.bfloat16)] * 4
        + [pltpu.VMEM((STEP, width, cols), jnp.float32), pltpu.SemaphoreType.DMA((8,))],
        compiler_params=pltpu.CompilerParams(vmem_limit_bytes=60 * 2**20),
        name="combine",
    )(*tables, *received, own, pool)


def per_device(fields, weights, source_block, target_block, area):
    width = weights.shape[1]
    cols = fields.shape[1]
    owned = area.shape[0] // width
    sectors = lax.axis_size("sector")
    groups_dev = target_block.shape[0]
    blocks = fields.reshape(-1, width, cols)
    sent = outgoing(blocks, weights, source_block, target_block, owned, sectors)
    arrived = exchange(
        sent[:FIRST], sent[FIRST], blocks, weights, source_block, area.reshape(owned, width), sectors,
        groups_dev,
    )
    ten, nine, eight = combine(arrived[4:8], arrived[8], arrived[:4], arrived[9])
    return ten.reshape(-1, cols), nine.reshape(-1, cols), eight.reshape(-1, cols)


def solution(mesh):
    in_specs = (
        P(("groups", "sector"), None),
        P("sector", None, None),
        P("sector"),
        P("sector"),
        P("sector"),
    )
    out_specs = (P(("groups", "sector"), None),) * 3
    return jax.shard_map(
        per_device, mesh=mesh, in_specs=in_specs, out_specs=out_specs, check_vma=False
    )
```

time: 64.2 us -> 57.4 us (0.89)
  Pallas kernels: 63 us -> 56.5 us
    pallas_call x1, Pallas kernels: 11.9 us -> 6.26 us  [outgoing(): pl.pallas_call(functools.partial(outgoing_kernel, sectors, owned, per_gro...]
    pallas_call x1, Pallas kernels: 42.7 us -> 41.1 us  [exchange(): pl.pallas_call(functools.partial(exchange_kernel, nb // groups_dev, secto...]
    pallas_call x1, Pallas kernels: 8.44 us -> 9.16 us  [combine(): pl.pallas_call(functools.partial(combine_kernel, table_size(owned)[0]), g...]
where the time goes in v3:
time: 57.4 us; the launch traced here: 57.1 us
  Pallas kernels  56.5 us (98%)
  between operations  0.65 us (1%)
    pallas_call x1, Pallas kernels, exchange(): pl.pallas_call(functools.partial(exchange_kernel, nb // groups_dev, secto...  41.1 us
    pallas_call x1, Pallas kernels, combine(): pl.pallas_call(functools.partial(combine_kernel, table_size(owned)[0]), g...  9.16 us
    pallas_call x1, Pallas kernels, outgoing(): pl.pallas_call(functools.partial(outgoing_kernel, sectors, owned, per_gro...  6.26 us

profile of v3, /device:TPU:1, one launch (start us, length us, event | category | flops | bytes accessed | tf_op | source)
XLA Modules:
  0.0 57.1 jit_solution(9159798513885457911)
XLA Ops:
  0.6 6.3 %outgoing.1 = (bf16[16,128,128]{2,1,0:T(8,128)(2,1)}, bf16[16,128,128]{2,1,0:T(8,128)(2,1)}, s32[768]{0:T(1024)}) custom-call(s32[320]{0:T(512)} %refs_3_.1, s32[80]{0:T(128)} %target_hbm.1, bf16[320,128,128]{2,1,0:T(8,128)(2,1)} %refs_4_.1, bf16[128,128,128]{2,1,0:T(8,128)(2,1)} %bitcast.5), custom_call_target="tpu_custom_call" | custom-call | tf_op jit(solution)/shard_map/outgoing/pallas_call | solution.py:142
  6.9 41.1 %exchange.1 = (bf16[16,128,128]{2,1,0:T(8,128)(2,1)}, bf16[16,128,128]{2,1,0:T(8,128)(2,1)}, bf16[16,128,128]{2,1,0:T(8,128)(2,1)}, bf16[16,128,128]{2,1,0:T(8,1...) custom-call(bf16[16,128,128]{2,1,0:T(8,128)(2,1)} %get-tuple-element, ...), custom_call_target="tpu_custom_call" | custom-call | tf_op jit(solution)/shard_map/exchange/pallas_call | solution.py:270
  48.0 9.2 %combine.1 = (bf16[64,128,128]{2,1,0:T(8,128)(2,1)}, f32[64,32,128]{2,1,0:T(8,128)}, f32[64,8,128]{2,1,0:T(8,128)}) custom-call(s32[768]{0:T(1024)} %get-tuple-element.22.refs_0_, s32[768]{0:T(1024)} %get-tuple-element.23.refs_1_, s32[768]{0:T(1024)} %get-tuple-element.24.refs_2_, s32[768]{0:T(1024)} %get-tuple-element.25.refs_3_, ...), custom_call_target="tpu_custom_call" | custom-call | tf_op jit(solution)/shard_map/combine/pallas_call | solution.py:348

commit v4 on v3

--- a/solution.py
+++ b/solution.py
@@ -10,7 +10,7 @@
 CAP = 16
 MOVES = (2, -2, 1, -1)
 CHUNK = 8
-STEP = 8
+STEP = 16
 FIRST = 2
 LANES = 128
 HBM = pl.BlockSpec(memory_space=pl.ANY)
@@ -301,65 +301,84 @@
 
 
 def combine_kernel(row, *refs):
-    tables, received_hbm, own, pool = refs[:4], refs[4:8], refs[8], refs[9]
-    ten, nine, eight = refs[10:13]
-    slots, received, acc, sem = refs[13:17], refs[17:21], refs[21], refs[22]
-
-    @pl.when(pl.program_id(0) == 0)
-    def _():
-        copies = [
-            pltpu.make_async_copy(table, slots[k], sem.at[k]) for k, table in enumerate(tables)
-        ] + [
-            pltpu.make_async_copy(part, received[k], sem.at[4 + k])
-            for k, part in enumerate(received_hbm)
-        ]
-        for copy in copies:
+    tables, received_hbm, own_hbm, pool_hbm = refs[:4], refs[4:8], refs[8], refs[9]
+    outs_hbm = refs[10:13]
+    slots, received, own, pool = refs[13:17], refs[17:21], refs[21], refs[22]
+    outs, sem, own_sem, pool_sem, out_sem = refs[23:26], refs[26], refs[27], refs[28], refs[29]
+    ten, nine, eight = outs
+    chunks = own_sem.shape[0]
+    step = own.shape[0] // chunks
+    n9 = nine.shape[1]
+
+    def part(source, place, c, semaphore):
+        rows = pl.ds(c * step, step)
+        return pltpu.make_async_copy(source.at[rows], place.at[rows], semaphore)
+
+    def results(c):
+        return [part(outs[i], outs_hbm[i], c, out_sem.at[3 * c + i]) for i in range(3)]
+
+    copies = [
+        pltpu.make_async_copy(table, slots[k], sem.at[k]) for k, table in enumerate(tables)
+    ] + [
+        pltpu.make_async_copy(block, received[k], sem.at[4 + k])
+        for k, block in enumerate(received_hbm)
+    ]
+    for copy in copies:
+        copy.start()
+    for c in range(chunks):
+        part(own_hbm, own, c, own_sem.at[c]).start()
+        part(pool_hbm, pool, c, pool_sem.at[c]).start()
+    for copy in copies:
+        copy.wait()
+
+    @pl.loop(0, chunks)
+    def _(c):
+        part(own_hbm, own, c, own_sem.at[c]).wait()
+        part(pool_hbm, pool, c, pool_sem.at[c]).wait()
+        for j in range(step):
+            t = c * step + j
+            total = own[t].astype(jnp.float32)
+            for k in range(4):
+                slot = slots[k][k * row + t]
+                value = received[k][jnp.maximum(slot, 0)].astype(jnp.float32)
+                total = total + jnp.where(slot >= 0, value, 0.0)
+            rounded = total.astype(jnp.bfloat16)
+            ten[t] = rounded
+            means = jnp.dot(pool[t], rounded, preferred_element_type=jnp.float32)
+            nine[t] = means[:n9]
+            eight[t] = means[n9:]
+        for copy in results(c):
             copy.start()
-        for copy in copies:
+
+    @pl.loop(0, chunks)
+    def _(c):
+        for copy in results(c):
             copy.wait()
-
-    base = pl.program_id(0) * STEP
-    n9 = nine.shape[1]
-    for j in range(STEP):
-        acc[j] = own[j].astype(jnp.float32)
-    for j in range(STEP):
-        for k in range(4):
-            slot = slots[k][k * row + base + j]
-
-            @pl.when(slot >= 0)
-            def _():
-                acc[j] += received[k][slot].astype(jnp.float32)
-
-    for j in range(STEP):
-        rounded = acc[j].astype(jnp.bfloat16)
-        ten[j] = rounded
-        means = jnp.dot(pool[j], rounded, preferred_element_type=jnp.float32)
-        nine[j] = means[:n9]
-        eight[j] = means[n9:]
 
 
 def combine(tables, own, received, pool):
     owned, width, cols = own.shape
-    n9, n8 = width // 4, width // 16
-
-    def rows(n):
-        return pl.BlockSpec((STEP, n, cols), lambda i: (i, 0, 0))
-
+    chunks = owned // STEP
+    outs = [
+        jax.ShapeDtypeStruct((owned, width, cols), jnp.bfloat16),
+        jax.ShapeDtypeStruct((owned, width // 4, cols), jnp.float32),
+        jax.ShapeDtypeStruct((owned, width // 16, cols), jnp.float32),
+    ]
     return pl.pallas_call(
         functools.partial(combine_kernel, table_size(owned)[0]),
-        grid=(owned // STEP,),
-        out_shape=[
-            jax.ShapeDtypeStruct((owned, width, cols), jnp.bfloat16),
-            jax.ShapeDtypeStruct((owned, n9, cols), jnp.float32),
-            jax.ShapeDtypeStruct((owned, n8, cols), jnp.float32),
-        ],
-        in_specs=[HBM] * 8
-        + [rows(width)]
-        + [pl.BlockSpec((STEP, n9 + n8, width), lambda i: (i, 0, 0))],
-        out_specs=[rows(width), rows(n9), rows(n8)],
+        out_shape=outs,
+        in_specs=[HBM] * 10,
+        out_specs=[HBM] * 3,
         scratch_shapes=[pltpu.SMEM(tables[0].shape, jnp.int32)] * 4
         + [pltpu.VMEM(received[0].shape, jnp.bfloat16)] * 4
-        + [pltpu.VMEM((STEP, width, cols), jnp.float32), pltpu.SemaphoreType.DMA((8,))],
+        + [pltpu.VMEM(own.shape, jnp.bfloat16), pltpu.VMEM(pool.shape, jnp.bfloat16)]
+        + [pltpu.VMEM(out.shape, out.dtype) for out in outs]
+        + [
+            pltpu.SemaphoreType.DMA((8,)),
+            pltpu.SemaphoreType.DMA((chunks,)),
+            pltpu.SemaphoreType.DMA((chunks,)),
+            pltpu.SemaphoreType.DMA((3 * chunks,)),
+        ],
         compiler_params=pltpu.CompilerParams(vmem_limit_bytes=60 * 2**20),
         name="combine",
     )(*tables, *received, own, pool)

time: 57.4 us -> 53.7 us (0.936)
  Pallas kernels: 56.5 us -> 53.3 us
    pallas_call x1, Pallas kernels: 9.16 us -> 5.9 us  [combine(): pl.pallas_call(functools.partial(combine_kernel, table_size(owned)[0]), o...]
    pallas_call x1, Pallas kernels: 41.1 us -> 42.1 us  [exchange(): pl.pallas_call(functools.partial(exchange_kernel, nb // groups_dev, secto...]
    pallas_call x1, Pallas kernels: 6.26 us -> 5.29 us  [outgoing(): pl.pallas_call(functools.partial(outgoing_kernel, sectors, owned, per_gro...]
where the time goes in v4:
time: 53.7 us; the launch traced here: 53.9 us
  Pallas kernels  53.3 us (99%)
  between operations  0.65 us (1%)
    pallas_call x1, Pallas kernels, exchange(): pl.pallas_call(functools.partial(exchange_kernel, nb // groups_dev, secto...  42.1 us
    pallas_call x1, Pallas kernels, combine(): pl.pallas_call(functools.partial(combine_kernel, table_size(owned)[0]), o...  5.9 us
    pallas_call x1, Pallas kernels, outgoing(): pl.pallas_call(functools.partial(outgoing_kernel, sectors, owned, per_gro...  5.29 us

profile of v4, /device:TPU:1, one launch (start us, length us, event | category | flops | bytes accessed | tf_op | source)
XLA Modules:
  0.0 53.9 jit_solution(3960002183824937979)
XLA Ops:
  0.6 5.3 %outgoing.1 = (bf16[16,128,128]{2,1,0:T(8,128)(2,1)}, bf16[16,128,128]{2,1,0:T(8,128)(2,1)}, s32[768]{0:T(1024)}) custom-call(s32[320]{0:T(512)} %refs_3_.1, s32[80]{0:T(128)} %target_hbm.1, bf16[320,128,128]{2,1,0:T(8,128)(2,1)} %refs_4_.1, bf16[128,128,128]{2,1,0:T(8,128)(2,1)} %bitcast.5), custom_call_target="tpu_custom_call" | custom-call | tf_op jit(solution)/shard_map/outgoing/pallas_call | solution.py:142
  5.9 42.1 %exchange.1 = (bf16[16,128,128]{2,1,0:T(8,128)(2,1)}, bf16[16,128,128]{2,1,0:T(8,128)(2,1)}, bf16[16,128,128]{2,1,0:T(8,128)(2,1)}, bf16[16,128,128]{2,1,0:T(8,1...) custom-call(bf16[16,128,128]{2,1,0:T(8,128)(2,1)} %get-tuple-element, ...), custom_call_target="tpu_custom_call" | custom-call | tf_op jit(solution)/shard_map/exchange/pallas_call | solution.py:270
  48.0 5.9 %combine.1 = (bf16[64,128,128]{2,1,0:T(8,128)(2,1)}, f32[64,32,128]{2,1,0:T(8,128)}, f32[64,8,128]{2,1,0:T(8,128)}) custom-call(s32[768]{0:T(1024)} %get-tuple-element.22.refs_0_, s32[768]{0:T(1024)} %get-tuple-element.23.refs_1_, s32[768]{0:T(1024)} %get-tuple-element.24.refs_2_, s32[768]{0:T(1024)} %get-tuple-element.25.refs_3_, ...), custom_call_target="tpu_custom_call" | custom-call | tf_op jit(solution)/shard_map/combine/pallas_call | solution.py:367

commit v5 on v4

--- a/solution.py
+++ b/solution.py
@@ -12,6 +12,7 @@
 CHUNK = 8
 STEP = 16
 FIRST = 2
+HEAD = 8
 LANES = 128
 HBM = pl.BlockSpec(memory_space=pl.ANY)
 
@@ -95,37 +96,37 @@
         table[chosen + slot] = g
         table[kind * width + local] = jnp.where(mine, g, rank)
 
-        @pl.when(kind < FIRST)
+        @pl.when((kind < FIRST) & (rank < HEAD))
         def _():
-            w_copy(g, slot).start()
+            w_copy(g, kind * HEAD + rank).start()
 
     table_copy = pltpu.make_async_copy(table, table_out, o_sem.at[FIRST])
     table_copy.start()
     for copy in fields_in:
         copy.wait()
 
-    unroll = 4
+    unroll = HEAD // 2
     copies = [table_copy]
     for k in range(FIRST):
 
-        @pl.loop(0, (count[k] + unroll - 1) // unroll)
+        @pl.loop(0, (jnp.minimum(count[k], HEAD) + unroll - 1) // unroll)
         def _(step):
             for r in range(unroll):
                 rank = step * unroll + r
-                slot = k * CAP + rank
 
                 @pl.when(rank < count[k])
                 def _():
-                    w_copy(table[chosen + slot], slot).wait()
+                    w_copy(table[chosen + k * CAP + rank], k * HEAD + rank).wait()
 
             for r in range(unroll):
-                slot = k * CAP + step * unroll + r
-                g = table[chosen + slot]
+                rank = step * unroll + r
+                slot = k * HEAD + rank
+                g = table[chosen + k * CAP + rank]
                 obuf[slot] = product(
                     wbuf, fbuf, source, slot * per_group, g * per_group, per_group
                 )
 
-        copy = pltpu.make_async_copy(obuf.at[pl.ds(CAP * k, CAP)], sends[k], o_sem.at[k])
+        copy = pltpu.make_async_copy(obuf.at[pl.ds(HEAD * k, HEAD)], sends[k], o_sem.at[k])
         copy.start()
         copies.append(copy)
     for copy in copies:
@@ -141,7 +142,7 @@
     _, chosen, tail = table_size(owned)
     return pl.pallas_call(
         functools.partial(outgoing_kernel, sectors, owned, per_group),
-        out_shape=[jax.ShapeDtypeStruct((CAP, *block), jnp.bfloat16)] * FIRST
+        out_shape=[jax.ShapeDtypeStruct((HEAD, *block), jnp.bfloat16)] * FIRST
         + [jax.ShapeDtypeStruct((chosen + tail,), jnp.int32)],
         in_specs=[HBM] * 4,
         out_specs=[HBM] * (FIRST + 1),
@@ -149,12 +150,12 @@
             pltpu.SMEM((nb,), jnp.int32),
             pltpu.SMEM((groups_dev,), jnp.int32),
             pltpu.SMEM((chosen + tail,), jnp.int32),
-            pltpu.VMEM((FIRST * CAP * per_group, width, width), jnp.bfloat16),
+            pltpu.VMEM((FIRST * HEAD * per_group, width, width), jnp.bfloat16),
             pltpu.VMEM(fields.shape, jnp.bfloat16),
-            pltpu.VMEM((FIRST * CAP, *block), jnp.bfloat16),
+            pltpu.VMEM((FIRST * HEAD, *block), jnp.bfloat16),
             pltpu.SMEM((len(MOVES) + 1,), jnp.int32),
             pltpu.SemaphoreType.DMA((2,)),
-            pltpu.SemaphoreType.DMA((FIRST * CAP,)),
+            pltpu.SemaphoreType.DMA((FIRST * HEAD,)),
             pltpu.SemaphoreType.DMA((4,)),
             pltpu.SemaphoreType.DMA((FIRST + 1,)),
         ],
@@ -168,9 +169,9 @@
     source_hbm, w_hbm, f_hbm, area = refs[FIRST + 1 : FIRST + 5]
     rest = refs[FIRST + 5 :]
     received, tables_out, own_out, pool = rest[:4], rest[4:8], rest[8], rest[9]
-    table, source, wbuf, fbuf, pbuf, obuf, near0, near1 = rest[10:18]
-    send_sem, recv_sem, i_sem, w_sem, f_sem, o_sem = rest[18:]
-    near = (near0, near1)
+    table, source, wbuf, fbuf, pbuf, obuf = rest[10:16]
+    later = rest[16:20]
+    send_sem, recv_sem, i_sem, w_sem, f_sem, o_sem = rest[20:]
     me = lax.axis_index("sector")
     kinds = len(MOVES)
     chunks = w_sem.shape[0]
@@ -207,7 +208,7 @@
             device_id_type=pl.DeviceIdType.MESH,
         )
 
-    moved = [remote(k, k, sends[k], received[k]) for k in range(FIRST)]
+    moved = [remote(k, k, sends[k], received[k].at[pl.ds(0, HEAD)]) for k in range(FIRST)]
     moved += [remote(kinds + k, k, table_hbm, tables_out[k]) for k in range(kinds)]
     for copy in moved:
         copy.start()
@@ -226,13 +227,15 @@
                 g = c * CHUNK + step * 4 + p
                 pbuf[g] = product(wbuf, fbuf, source, g * per_group, g * per_group, per_group)
 
-    for k in range(FIRST, kinds):
-
-        @pl.loop(0, CAP)
-        def _(rank):
-            near[k - FIRST][rank] = pbuf[table[chosen + k * CAP + rank]]
-
-        moved.append(remote(k, k, near[k - FIRST], received[k]))
+    for k in range(kinds):
+        done = HEAD if k < FIRST else 0
+
+        @pl.loop(0, CAP - done)
+        def _(i):
+            later[k][i] = pbuf[table[chosen + k * CAP + done + i]]
+
+        rows = pl.ds(done, CAP - done)
+        moved.append(remote(2 * kinds + k, k, later[k], received[k].at[rows]))
         moved[-1].start()
 
     @pl.loop(0, owned)
@@ -284,10 +287,14 @@
             pltpu.VMEM(fields.shape, jnp.bfloat16),
             pltpu.VMEM((groups_dev, *block), jnp.bfloat16),
             pltpu.VMEM((owned, *block), jnp.bfloat16),
-            pltpu.VMEM((CAP, *block), jnp.bfloat16),
-            pltpu.VMEM((CAP, *block), jnp.bfloat16),
-            pltpu.SemaphoreType.DMA((2 * kinds,)),
-            pltpu.SemaphoreType.DMA((2 * kinds,)),
+        ]
+        + [
+            pltpu.VMEM((CAP - (HEAD if k < FIRST else 0), *block), jnp.bfloat16)
+            for k in range(kinds)
+        ]
+        + [
+            pltpu.SemaphoreType.DMA((3 * kinds,)),
+            pltpu.SemaphoreType.DMA((3 * kinds,)),
             pltpu.SemaphoreType.DMA((2,)),
             pltpu.SemaphoreType.DMA((groups_dev // CHUNK,)),
             pltpu.SemaphoreType.DMA((4,)),

time: 53.7 us -> 52.8 us (0.983)
  Pallas kernels: 53.3 us -> 51.9 us
    pallas_call x1, Pallas kernels: 5.29 us -> 4.4 us  [outgoing(): pl.pallas_call(functools.partial(outgoing_kernel, sectors, owned, per_gro...]
where the time goes in v5:
time: 52.8 us; the launch traced here: 52.6 us
  Pallas kernels  51.9 us (98%)
  between operations  0.65 us (1%)
    pallas_call x1, Pallas kernels, exchange(): pl.pallas_call(functools.partial(exchange_kernel, nb // groups_dev, secto...  41.6 us
    pallas_call x1, Pallas kernels, combine(): pl.pallas_call(functools.partial(combine_kernel, table_size(owned)[0]), o...  5.9 us
    pallas_call x1, Pallas kernels, outgoing(): pl.pallas_call(functools.partial(outgoing_kernel, sectors, owned, per_gro...  4.4 us

profile of v5, /device:TPU:1, one launch (start us, length us, event | category | flops | bytes accessed | tf_op | source)
XLA Modules:
  0.0 52.6 jit_solution(6245853405477468822)
XLA Ops:
  0.6 4.4 %outgoing.1 = (bf16[8,128,128]{2,1,0:T(8,128)(2,1)}, bf16[8,128,128]{2,1,0:T(8,128)(2,1)}, s32[768]{0:T(1024)}) custom-call(s32[320]{0:T(512)} %refs_3_.1, s32[80]{0:T(128)} %target_hbm.1, bf16[320,128,128]{2,1,0:T(8,128)(2,1)} %refs_4_.1, bf16[128,128,128]{2,1,0:T(8,128)(2,1)} %bitcast.5), custom_call_target="tpu_custom_call" | custom-call | tf_op jit(solution)/shard_map/outgoing/pallas_call | solution.py:143
  5.0 41.6 %exchange.1 = (bf16[16,128,128]{2,1,0:T(8,128)(2,1)}, bf16[16,128,128]{2,1,0:T(8,128)(2,1)}, bf16[16,128,128]{2,1,0:T(8,128)(2,1)}, bf16[16,128,128]{2,1,0:T(8,1...) custom-call(bf16[8,128,128]{2,1,0:T(8,128)(2,1)} %get-tuple-element., ...), custom_call_target="tpu_custom_call" | custom-call | tf_op jit(solution)/shard_map/exchange/pallas_call | solution.py:273
  46.7 5.9 %combine.1 = (bf16[64,128,128]{2,1,0:T(8,128)(2,1)}, f32[64,32,128]{2,1,0:T(8,128)}, f32[64,8,128]{2,1,0:T(8,128)}) custom-call(s32[768]{0:T(1024)} %get-tuple-element.22.refs_0_, s32[768]{0:T(1024)} %get-tuple-element.23.refs_1_, s32[768]{0:T(1024)} %get-tuple-element.24.refs_2_, s32[768]{0:T(1024)} %get-tuple-element.25.refs_3_, ...), custom_call_target="tpu_custom_call" | custom-call | tf_op jit(solution)/shard_map/combine/pallas_call | solution.py:374

commit v6 on v5

--- a/solution.py
+++ b/solution.py
@@ -105,7 +105,7 @@
     for copy in fields_in:
         copy.wait()
 
-    unroll = HEAD // 2
+    unroll = HEAD
     copies = [table_copy]
     for k in range(FIRST):
 

time: 52.8 us -> 52.7 us (level)
  no operation moved by 1% of the time
where the time goes in v6:
time: 52.7 us; the launch traced here: 52.6 us
  Pallas kernels  52 us (99%)
  between operations  0.65 us (1%)
    pallas_call x1, Pallas kernels, exchange(): pl.pallas_call(functools.partial(exchange_kernel, nb // groups_dev, secto...  41.5 us
    pallas_call x1, Pallas kernels, combine(): pl.pallas_call(functools.partial(combine_kernel, table_size(owned)[0]), o...  5.9 us
    pallas_call x1, Pallas kernels, outgoing(): pl.pallas_call(functools.partial(outgoing_kernel, sectors, owned, per_gro...  4.61 us

profile of v6, /device:TPU:1, one launch (start us, length us, event | category | flops | bytes accessed | tf_op | source)
XLA Modules:
  0.0 52.6 jit_solution(305571493062641210)
XLA Ops:
  0.6 4.6 %outgoing.1 = (bf16[8,128,128]{2,1,0:T(8,128)(2,1)}, bf16[8,128,128]{2,1,0:T(8,128)(2,1)}, s32[768]{0:T(1024)}) custom-call(s32[320]{0:T(512)} %refs_3_.1, s32[80]{0:T(128)} %target_hbm.1, bf16[320,128,128]{2,1,0:T(8,128)(2,1)} %refs_4_.1, bf16[128,128,128]{2,1,0:T(8,128)(2,1)} %bitcast.5), custom_call_target="tpu_custom_call" | custom-call | tf_op jit(solution)/shard_map/outgoing/pallas_call | solution.py:143
  5.2 41.5 %exchange.1 = (bf16[16,128,128]{2,1,0:T(8,128)(2,1)}, bf16[16,128,128]{2,1,0:T(8,128)(2,1)}, bf16[16,128,128]{2,1,0:T(8,128)(2,1)}, bf16[16,128,128]{2,1,0:T(8,1...) custom-call(bf16[8,128,128]{2,1,0:T(8,128)(2,1)} %get-tuple-element., ...), custom_call_target="tpu_custom_call" | custom-call | tf_op jit(solution)/shard_map/exchange/pallas_call | solution.py:273
  46.7 5.9 %combine.1 = (bf16[64,128,128]{2,1,0:T(8,128)(2,1)}, f32[64,32,128]{2,1,0:T(8,128)}, f32[64,8,128]{2,1,0:T(8,128)}) custom-call(s32[768]{0:T(1024)} %get-tuple-element.22.refs_0_, s32[768]{0:T(1024)} %get-tuple-element.23.refs_1_, s32[768]{0:T(1024)} %get-tuple-element.24.refs_2_, s32[768]{0:T(1024)} %get-tuple-element.25.refs_3_, ...), custom_call_target="tpu_custom_call" | custom-call | tf_op jit(solution)/shard_map/combine/pallas_call | solution.py:374
